TPU v7x, 32 devices: a whole 2x2x4 slice. The times are simulated.
32 devices in a mesh: slab: 2 (over y), gy: 4 (over z), gx: 4 (over x, core).
Axes of the slice: x: 2, y: 2, z: 4, core: 2. Of those that a mesh axis runs over, the one named last changes fastest.
Arguments:
- volume: float32 [8, 256, 1024], P(None, ('slab', 'gy'), 'gx'), parts along dimension 1, may hold values from -8 to 8
- tissue_mask: int32 [2, 32, 128], P(None, ('slab', 'gy'), 'gx'), parts along dimension 1, may hold values from 0 to 1
- smoothing: float32 [1], replicated, may hold values from 0.7 to 1.4
Outputs:
- filtered: float32 [8, 256, 1024], P(None, ('slab', 'gy'), 'gx'), parts along dimension 1
There are 2 independent parts, one for each index of `slab`. A program takes and returns all parts, laid end to end along the dimension named above; an argument that names none is the same for every part. Nothing has to cross between parts.
All inputs are finite; a program needn't handle non-finite values.
Results may differ from a plain program's by a relative error of at most 0.00002.
Values sent between devices are 32-bit elements; how exact they have to be, the bound alone decides.
A program may use at most 64 MiB of HBM per device.

v0:
```python
import functools

import jax
import jax.numpy as jnp
from jax import lax
from jax.experimental import pallas as pl
from jax.experimental.pallas import tpu as pltpu
from jax.sharding import PartitionSpec as P

MESH = pl.DeviceIdType.MESH
PHASES = ((0, 2), (0, 1), (1, 2))
LOG2E = 1.4426950408889634
SHIFTS = (-9, -8, -7, -1, 0, 1, 7, 8, 9)
DIRS = ((1, 0), (-1, 0), (0, 1), (0, -1), (1, 1), (1, -1), (-1, 1), (-1, -1))


def kernel(
    ny, nx, smooth_ref, vol_hbm, mask_hbm, out_ref, vol_ref, mask_ref, cubes,
    mid, base, shifted, tissue, tissvals, numer, denom, own_tiss, near_tiss, wide_tiss,
    rows_in, row_in, row_out, pack_out, pack_in, corner_in, edge, sums,
    load_sem, sum_send, sum_recv, halo_send, halo_recv,
):
    depth, rows, cols = vol_ref.shape
    lanes = 128
    tiles = cols // lanes
    blocks_z, blocks_y, blocks_x = mask_ref.shape
    padded = shifted.shape[3]
    peers = ny * nx
    half = depth // 2
    phases = [(low * half, high * half) for low, high in PHASES]
    gy, gx = lax.axis_index("gy"), lax.axis_index("gx")
    me = gy * nx + gx

    barrier = pltpu.get_barrier_semaphore()
    for k in range(1, peers):
        flat = lax.rem(me + k, peers)
        pl.semaphore_signal(
            barrier, inc=1, device_id={"gy": flat // nx, "gx": lax.rem(flat, nx)}, device_id_type=MESH
        )

    loads = [
        pltpu.make_async_copy(mask_hbm, mask_ref, load_sem.at[0]),
        pltpu.make_async_copy(vol_hbm, vol_ref, load_sem.at[1]),
    ]
    for load in loads:
        load.start()

    def exists(dy, dx):
        found = None
        for step, pos, count in ((dy, gy, ny), (dx, gx, nx)):
            if step == 0:
                continue
            here = pos < count - 1 if step > 0 else pos > 0
            found = here if found is None else jnp.logical_and(found, here)
        return found

    def lane_group(shape):
        return lax.broadcasted_iota(jnp.int32, shape, 1) // 16

    def make_packs(src, it):
        group = lane_group((rows, lanes))
        right = jnp.zeros((rows, lanes), jnp.float32)
        left = right
        for z in range(*phases[it]):
            high = pltpu.roll(src[z, :, cols - lanes : cols], (16 * z + 16) % lanes, 1)
            right = jnp.where(group == z, high, right)
            low = src[z, :, 0:lanes]
            if z:
                low = pltpu.roll(low, 16 * z, 1)
            left = jnp.where(group == z, low, left)
            row_out[it, 0, z : z + 1] = src[z, rows - 9 : rows - 8, :]
            row_out[it, 1, z : z + 1] = src[z, 8:9, :]
        pack_out[it, 0] = right
        pack_out[it, 1] = left

    def copies(src, it, d):
        dy, dx = DIRS[d]
        pairs = []
        if dx == 0:
            start = rows - 8 if dy > 0 else 0
            low, high = phases[it]
            pairs.append((src.at[low:high, start : start + 8, :], rows_in.at[it, d, low:high]))
            pairs.append((row_out.at[it, d], row_in.at[it, d]))
        elif dy == 0:
            pairs.append((pack_out.at[it, d - 2], pack_in.at[it, d - 2]))
        else:
            start = rows - 16 if dy > 0 else 0
            pairs.append(
                (pack_out.at[it, 0 if dx > 0 else 1, start : start + 16], corner_in.at[it, d - 4])
            )
        if it == 0:
            at = {1: slice(cols - lanes, cols), -1: slice(0, lanes), 0: slice(0, cols)}[dx]
            pairs.append((own_tiss.at[:, at], near_tiss.at[d, :, at]))
        return [
            pltpu.make_async_remote_copy(
                src_ref=a,
                dst_ref=b,
                send_sem=halo_send.at[it, d, j],
                recv_sem=halo_recv.at[it, d, j],
                device_id={"gy": gy + dy, "gx": gx + dx},
                device_id_type=MESH,
            )
            for j, (a, b) in enumerate(pairs)
        ]

    def clear_missing(it):
        for d, (dy, dx) in enumerate(DIRS):

            @pl.when(jnp.logical_not(exists(-dy, -dx)))
            def _():
                if dx == 0:
                    rows_in[it, d] = jnp.zeros(rows_in.shape[2:], jnp.float32)
                    row_in[it, d] = jnp.zeros(row_in.shape[2:], jnp.float32)
                elif dy == 0:
                    pack_in[it, d - 2] = jnp.zeros(pack_in.shape[2:], jnp.float32)
                else:
                    corner_in[it, d - 4] = jnp.zeros(corner_in.shape[2:], jnp.float32)
                if it == 0:
                    near_tiss[d] = jnp.zeros(near_tiss.shape[1:], jnp.float32)

    def start_halo(src, it):
        for d, (dy, dx) in enumerate(DIRS):

            @pl.when(exists(dy, dx))
            def _():
                for copy in copies(src, it, d):
                    copy.start()

    def wait_halo(src, it):
        for d, (dy, dx) in enumerate(DIRS):

            @pl.when(exists(-dy, -dx))
            def _():
                for copy in copies(src, it, d):
                    copy.wait_recv()

    def wait_sent(src, it):
        for d, (dy, dx) in enumerate(DIRS):

            @pl.when(exists(dy, dx))
            def _():
                for copy in copies(src, it, d):
                    copy.wait_send()

    def sum_copy(k):
        flat = lax.rem(me + k, peers)
        return pltpu.make_async_remote_copy(
            src_ref=sums.at[0],
            dst_ref=sums.at[k],
            send_sem=sum_send.at[k],
            recv_sem=sum_recv.at[k],
            device_id={"gy": flat // nx, "gx": lax.rem(flat, nx)},
            device_id_type=MESH,
        )

    def spread_tissue():
        for zb in range(blocks_z):
            first = zb * blocks_y
            wide_tiss[zb, 1 : 1 + blocks_y, lanes : lanes + cols] = own_tiss[first : first + blocks_y]
            wide_tiss[zb, 1 : 1 + blocks_y, 0:lanes] = near_tiss[2, first : first + blocks_y, cols - lanes : cols]
            wide_tiss[zb, 1 : 1 + blocks_y, lanes + cols :] = near_tiss[3, first : first + blocks_y, 0:lanes]
            for row, source, at in ((0, (0, 4, 5), first + blocks_y - 1), (1 + blocks_y, (1, 6, 7), first)):
                mid_d, left_d, right_d = source
                wide_tiss[zb, row : row + 1, lanes : lanes + cols] = near_tiss[mid_d, at : at + 1, :]
                wide_tiss[zb, row : row + 1, 0:lanes] = near_tiss[left_d, at : at + 1, cols - lanes : cols]
                wide_tiss[zb, row : row + 1, lanes + cols :] = near_tiss[right_d, at : at + 1, 0:lanes]
            for ci, c in enumerate((-8, 0, 8)):
                moved = wide_tiss[zb, :, lanes + c : lanes + c + cols]
                for lt in range(tiles):
                    for rb in range(blocks_y + 2):
                        line = moved[rb : rb + 1, lt * lanes : (lt + 1) * lanes]
                        tissue[ci, lt, zb, rb * 8 : rb * 8 + 8] = jnp.broadcast_to(line, (8, lanes))

    def fill_centre(src, it):
        for z in range(*phases[it]):
            base[z, 9 : 9 + rows] = src[z]

    def fill_shifted(it):
        for z in range(*phases[it]):
            base[z, 0:1] = row_in[it, 0, z : z + 1]
            base[z, 1:9] = rows_in[it, 0, z]
            base[z, 9 + rows : 17 + rows] = rows_in[it, 1, z]
            base[z, 17 + rows : 18 + rows] = row_in[it, 1, z : z + 1]
        for side, (top, bottom) in enumerate(((0, 2), (1, 3))):
            edge[side, 0:9] = corner_in[it, top, 7:16]
            edge[side, 9 : 9 + rows] = pack_in[it, side]
            edge[side, 9 + rows : 18 + rows] = corner_in[it, bottom, 0:9]
        for z in range(*phases[it]):
            left = edge[0]
            if (112 - 16 * z) % lanes:
                left = pltpu.roll(left, (112 - 16 * z) % lanes, 1)
            right = edge[1]
            if z:
                right = pltpu.roll(right, (-16 * z) % lanes, 1)
            whole = jnp.concatenate([left, base[z], right], axis=1)
            for si, d in enumerate(SHIFTS):
                part = whole[:, lanes + d : lanes + d + cols]
                for lt in range(tiles):
                    shifted[si, lt, z] = part[:, lt * lanes : (lt + 1) * lanes]
        for ci in range(3):
            for lt in range(tiles):
                for z in range(*phases[it]):
                    vals = shifted[3 * ci + 1, lt, z, 1 : 17 + rows]
                    tissvals[ci, lt, z] = vals * tissue[ci, lt, z // 4]

    def clear_sums():
        numer[...] = jnp.zeros(numer.shape, jnp.float32)
        denom[...] = jnp.zeros(denom.shape, jnp.float32)

    def gather(passes, scale):
        span = rows + 8

        def body(step, carry):
            lt = step // 3
            bi = lax.rem(step, 3)
            row = pl.multiple_of(bi * 8, 8)

            def squares(zi, a, ci):
                inside, moved = 0 <= zi < depth, 0 <= zi + a < depth
                if not inside and not moved:
                    return None
                total = None
                for k in range(3):
                    if inside:
                        differ = shifted[3 + k, lt, zi, 8 : 8 + span]
                    if moved:
                        other = shifted[3 * ci + k, lt, zi + a, pl.ds(row, span)]
                        differ = differ - other if inside else other
                    part = differ * differ
                    total = part if total is None else total + part
                return total

            slot = 0
            for ci in range(3):
                for a, low, high in passes:
                    before, here = squares(low - 1, a, ci), squares(low, a, ci)
                    pair = here if before is None else before + here
                    for z in range(low, high):
                        after = squares(z + 1, a, ci)
                        cube = pair if after is None else pair + after
                        cubes[slot] = cube
                        distance = cube[0:rows] + cubes[slot, 1 : rows + 1] + cubes[slot, 2 : rows + 2]
                        slot += 1
                        weight = jnp.exp2(distance * scale)
                        numer[lt, z] += weight * tissvals[ci, lt, z + a, pl.ds(row, rows)]
                        denom[lt, z] += weight * tissue[ci, lt, (z + a) // 4, pl.ds(row, rows)]
                        pair = here if after is None else here + after
                        here = after
            return carry

        lax.fori_loop(0, tiles * 3, body, 0)

    def finish(src, dst, low, high):
        for lt in range(tiles):
            for z in range(low, high):
                flag = tissue[1, lt, z // 4, 8 : 8 + rows]
                at = slice(lt * lanes, (lt + 1) * lanes)
                dst[z, :, at] = (
                    flag * numer[lt, z] / (denom[lt, z] + 1.0 - flag) + (1.0 - flag) * src[z, :, at]
                )

    loads[0].wait()
    spread = (
        lax.broadcasted_iota(jnp.int32, (blocks_x, cols), 1) // 8
        == lax.broadcasted_iota(jnp.int32, (blocks_x, cols), 0)
    ).astype(jnp.float32)
    for zb in range(blocks_z):
        flags = mask_ref[zb].astype(jnp.float32)
        own_tiss[zb * blocks_y : (zb + 1) * blocks_y] = jnp.dot(
            flags, spread, preferred_element_type=jnp.float32
        )
    loads[1].wait()
    total = jnp.zeros((8, cols), jnp.float32)
    count = jnp.zeros((8, cols), jnp.float32)
    for z in range(1, depth - 1):
        residual = vol_ref[z] - 0.5 * (vol_ref[z - 1] + vol_ref[z + 1])
        for yb in range(blocks_y):
            line = (z // 4) * blocks_y + yb
            flag = jnp.broadcast_to(own_tiss[line : line + 1], (8, cols))
            piece = residual[8 * yb : 8 * yb + 8]
            total = total + flag * piece * piece
            count = count + flag
    total = jnp.sum(total, axis=0, keepdims=True)
    count = jnp.sum(count, axis=0, keepdims=True)
    total = functools.reduce(jnp.add, [total[:, i * lanes : (i + 1) * lanes] for i in range(tiles)])
    count = functools.reduce(jnp.add, [count[:, i * lanes : (i + 1) * lanes] for i in range(tiles)])
    lane = lax.broadcasted_iota(jnp.int32, (1, lanes), 1)
    sums[0] = jnp.where(
        lane < lanes // 2,
        jnp.sum(total, axis=1, keepdims=True),
        jnp.sum(count, axis=1, keepdims=True),
    )
    make_packs(vol_ref, 0)
    pl.semaphore_wait(barrier, peers - 1)
    for k in range(1, peers):
        sum_copy(k).start()
    start_halo(vol_ref, 0)
    for it in range(len(PHASES)):
        clear_missing(it)
    fill_centre(vol_ref, 0)
    clear_sums()
    wait_halo(vol_ref, 0)
    spread_tissue()
    fill_shifted(0)
    for k in range(1, peers):
        sum_copy(k).wait_recv()
    everything = sums[0]
    for k in range(1, peers):
        everything = everything + sums[k]
    summed = everything[:, 0:1] * (2.0 / 3.0)
    tissue_count = everything[:, lanes // 2 : lanes // 2 + 1]
    variance = summed / jnp.maximum(tissue_count, 1.0) + 1e-05
    width = 54.0 * smooth_ref[0] * smooth_ref[0]
    scale = jnp.broadcast_to(-LOG2E / (width * variance), (rows, lanes))
    for it, passes in ((1, ((0, 0, half), (4, 0, half))), (2, ((0, half, depth), (-4, half, depth)))):
        gather(passes, scale)
        finish(vol_ref, mid, *phases[it])
        make_packs(mid, it)
        start_halo(mid, it)
    clear_sums()
    fill_centre(mid, 1)
    wait_halo(mid, 1)
    fill_shifted(1)
    gather(((0, 0, half - 1),), scale)
    fill_centre(mid, 2)
    wait_halo(mid, 2)
    fill_shifted(2)
    gather(((0, half - 1, depth), (4, 0, half), (-4, half, depth)), scale)
    finish(mid, out_ref, 0, depth)
    wait_sent(vol_ref, 0)
    wait_sent(mid, 1)
    wait_sent(mid, 2)
    for k in range(1, peers):
        sum_copy(k).wait_send()


def on_device(volume, tissue_mask, smoothing):
    ny, nx = lax.axis_size("gy"), lax.axis_size("gx")
    depth, rows, cols = volume.shape
    blocks_z, blocks_y, blocks_x = tissue_mask.shape
    lanes = 128
    tiles = cols // lanes
    padded = -(-(rows + 18) // 8) * 8
    flag_rows = -(-(blocks_y + 2) // 8) * 8
    f32 = jnp.float32
    vmem = pl.BlockSpec(memory_space=pltpu.VMEM)
    anywhere = pl.BlockSpec(memory_space=pltpu.HBM)
    return pl.pallas_call(
        functools.partial(kernel, ny, nx),
        out_shape=jax.ShapeDtypeStruct(volume.shape, f32),
        in_specs=[pl.BlockSpec(memory_space=pltpu.SMEM), anywhere, anywhere],
        out_specs=vmem,
        scratch_shapes=[
            pltpu.VMEM((depth, rows, cols), f32),
            pltpu.VMEM((blocks_z, blocks_y, blocks_x), jnp.int32),
            pltpu.VMEM((60, rows + 8, lanes), f32),
            pltpu.VMEM((depth, rows, cols), f32),
            pltpu.VMEM((depth, padded, cols), f32),
            pltpu.VMEM((len(SHIFTS), tiles, depth, padded, lanes), f32),
            pltpu.VMEM((3, tiles, blocks_z, rows + 16, lanes), f32),
            pltpu.VMEM((3, tiles, depth, rows + 16, lanes), f32),
            pltpu.VMEM((tiles, depth, rows, lanes), f32),
            pltpu.VMEM((tiles, depth, rows, lanes), f32),
            pltpu.VMEM((blocks_z * blocks_y, cols), f32),
            pltpu.VMEM((len(DIRS), blocks_z * blocks_y, cols), f32),
            pltpu.VMEM((blocks_z, flag_rows, cols + 2 * lanes), f32),
            pltpu.VMEM((len(PHASES), 2, depth, 8, cols), f32),
            pltpu.VMEM((len(PHASES), 2, depth, cols), f32),
            pltpu.VMEM((len(PHASES), 2, depth, cols), f32),
            pltpu.VMEM((len(PHASES), 2, rows, lanes), f32),
            pltpu.VMEM((len(PHASES), 2, rows, lanes), f32),
            pltpu.VMEM((len(PHASES), 4, 16, lanes), f32),
            pltpu.VMEM((2, padded, lanes), f32),
            pltpu.VMEM((ny * nx, 1, lanes), f32),
            pltpu.SemaphoreType.DMA((2,)),
            pltpu.SemaphoreType.DMA((ny * nx,)),
            pltpu.SemaphoreType.DMA((ny * nx,)),
            pltpu.SemaphoreType.DMA((len(PHASES), len(DIRS), 3)),
            pltpu.SemaphoreType.DMA((len(PHASES), len(DIRS), 3)),
        ],
        compiler_params=pltpu.CompilerParams(
            collective_id=0, has_side_effects=True, vmem_limit_bytes=16 * 2**20
        ),
    )(
        smoothing,
        pltpu.with_memory_space_constraint(volume, pltpu.HBM),
        pltpu.with_memory_space_constraint(tissue_mask, pltpu.HBM),
    )


def solution(mesh):
    placed = (P(None, ("slab", "gy"), "gx"), P(None, ("slab", "gy"), "gx"), P())
    return jax.shard_map(
        on_device,
        mesh=mesh,
        in_specs=placed,
        out_specs=P(None, ("slab", "gy"), "gx"),
        check_vma=False,
    )
```

profile of v0, /device:TPU:0, one launch (start us, length us, event | category | flops | bytes accessed | tf_op | source)
XLA Modules:
  0.0 29.4 jit_solution(9262901851917289762)
XLA Ops:
  0.7 28.0 %shard_map.37 = f32[8,32,256]{2,1,0:T(8,128)S(1)} custom-call(f32[1]{0:T(128)S(6)} %copy.5.smooth_ref, f32[8,32,256]{2,1,0:T(8,128)} %vol_hbm.1, s32[2,4,32]{2,1,0:T(4,128)} %mask_hbm.1), custom_call_target="tpu_custom_call" | custom-call | tf_op jit(solution)/shard_map/pallas_call | solution.py:348
  28.7 0.7 %copy.6 = f32[8,32,256]{2,1,0:T(8,128)} copy(f32[8,32,256]{2,1,0:T(8,128)S(1)} %shard_map.37) | data formatting | bytes 524288
where the time goes:
time: 29.6 us; the launch traced here: 29.4 us
  Pallas kernels  28 us (95%)
  local copies, waits for them, and re-layouts  0.71 us (2%)
  between operations  0.66 us (2%)
    pallas_call x1, Pallas kernels, on_device(): pl.pallas_call(functools.partial(kernel, ny, nx), out_shape=jax.ShapeDtyp...  28 us
    unnamed x1, local copies, waits for them, and re-layouts  0.71 us

commit v1 on v0

v1 whole, which is shorter than its diff:
```python
import functools

import jax
import jax.numpy as jnp
from jax import lax
from jax.experimental import pallas as pl
from jax.experimental.pallas import tpu as pltpu
from jax.sharding import PartitionSpec as P

MESH = pl.DeviceIdType.MESH
ITERS = 2
LOG2E = 1.4426950408889634
BIG = 1e30
DIRS = ((1, 0), (-1, 0), (0, 1), (0, -1), (1, 1), (1, -1), (-1, 1), (-1, -1))
LEVEL = ((0, 0, 8), (0, 8, 8), (0, -8, 8), (0, 8, 0))
CROSS = (
    (4, 0, 8), (4, 8, 8), (4, -8, 8), (-4, 0, 8), (-4, 8, 8), (-4, -8, 8), (4, 0, 0), (4, 8, 0), (4, -8, 0)
)
PAD = 16
SLOTS = 32


def kernel(
    ny, nx, smooth_ref, vol_hbm, mask_hbm, out_ref, vol_ref, mask_ref, mid, vals, packs, squares,
    cubes, acc, pacc, pens, ppens, own_tiss, near_tiss, wide_tiss,
    rows_in, row_in, row_out, pack_out, pack_in, side_in, corner_in, sums,
    load_sem, sum_send, sum_recv, halo_send, halo_recv,
):
    depth, rows, cols = vol_ref.shape
    lanes = 128
    blocks_z, blocks_y, blocks_x = mask_ref.shape
    nb = rows // 8
    step = lanes - 2
    peers = ny * nx
    gy, gx = lax.axis_index("gy"), lax.axis_index("gx")
    me = gy * nx + gx

    barrier = pltpu.get_barrier_semaphore()
    for k in range(1, peers):
        flat = lax.rem(me + k, peers)
        pl.semaphore_signal(
            barrier, inc=1, device_id={"gy": flat // nx, "gx": lax.rem(flat, nx)}, device_id_type=MESH
        )

    loads = [
        pltpu.make_async_copy(mask_hbm, mask_ref, load_sem.at[0]),
        pltpu.make_async_copy(vol_hbm, vol_ref, load_sem.at[1]),
    ]
    for load in loads:
        load.start()

    def lane_of(n):
        return lax.broadcasted_iota(jnp.int32, (n, lanes), 1)

    def exists(dy, dx):
        found = None
        for move, pos, count in ((dy, gy, ny), (dx, gx, nx)):
            if move == 0:
                continue
            here = pos < count - 1 if move > 0 else pos > 0
            found = here if found is None else jnp.logical_and(found, here)
        return found

    def roll(x, shift):
        shift = shift % lanes
        return pltpu.roll(x, shift, 1) if shift else x

    def make_packs(src, it):
        group = lane_of(rows) // 16
        right = jnp.zeros((rows, lanes), jnp.float32)
        left = right
        for z in range(depth):
            right = jnp.where(group == z, roll(src[z, :, cols - lanes : cols], 16 * z + 9), right)
            left = jnp.where(group == z, roll(src[z, :, 0:lanes], 16 * z), left)
            row_out[it, 0, z : z + 1] = src[z, rows - 9 : rows - 8, :]
            row_out[it, 1, z : z + 1] = src[z, 8:9, :]
        pack_out[it, 0] = right
        pack_out[it, 1] = left

    def copies(src, it, d):
        dy, dx = DIRS[d]
        pairs = []
        if dx == 0:
            start = rows - 8 if dy > 0 else 0
            pairs.append((src.at[:, start : start + 8, :], rows_in.at[it, d]))
            pairs.append((row_out.at[it, d], row_in.at[it, d]))
            start = rows - 16 if dy > 0 else 0
            pairs.append((pack_out.at[it, :, start : start + 16], side_in.at[it, d]))
        elif dy == 0:
            pairs.append((pack_out.at[it, d - 2], pack_in.at[it, d - 2]))
        else:
            start = rows - 16 if dy > 0 else 0
            pairs.append((pack_out.at[it, 0 if dx > 0 else 1, start : start + 16], corner_in.at[it, d - 4]))
        if it == 0:
            at = {1: slice(cols - lanes, cols), -1: slice(0, lanes), 0: slice(0, cols)}[dx]
            pairs.append((own_tiss.at[:, at], near_tiss.at[d, :, at]))
        return [
            pltpu.make_async_remote_copy(
                src_ref=a,
                dst_ref=b,
                send_sem=halo_send.at[it, d, j],
                recv_sem=halo_recv.at[it, d, j],
                device_id={"gy": gy + dy, "gx": gx + dx},
                device_id_type=MESH,
            )
            for j, (a, b) in enumerate(pairs)
        ]

    def clear_missing(it):
        for d, (dy, dx) in enumerate(DIRS):

            @pl.when(jnp.logical_not(exists(-dy, -dx)))
            def _():
                if dx == 0:
                    rows_in[it, d] = jnp.zeros(rows_in.shape[2:], jnp.float32)
                    row_in[it, d] = jnp.zeros(row_in.shape[2:], jnp.float32)
                    side_in[it, d] = jnp.zeros(side_in.shape[2:], jnp.float32)
                elif dy == 0:
                    pack_in[it, d - 2] = jnp.zeros(pack_in.shape[2:], jnp.float32)
                else:
                    corner_in[it, d - 4] = jnp.zeros(corner_in.shape[2:], jnp.float32)
                if it == 0:
                    near_tiss[d] = jnp.zeros(near_tiss.shape[1:], jnp.float32)

    def start_halo(src, it):
        for d, (dy, dx) in enumerate(DIRS):

            @pl.when(exists(dy, dx))
            def _():
                for copy in copies(src, it, d):
                    copy.start()

    def wait_halo(src, it):
        for d, (dy, dx) in enumerate(DIRS):

            @pl.when(exists(-dy, -dx))
            def _():
                for copy in copies(src, it, d):
                    copy.wait_recv()

    def wait_sent(src, it):
        for d, (dy, dx) in enumerate(DIRS):

            @pl.when(exists(dy, dx))
            def _():
                for copy in copies(src, it, d):
                    copy.wait_send()

    def sum_copy(k):
        flat = lax.rem(me + k, peers)
        return pltpu.make_async_remote_copy(
            src_ref=sums.at[0],
            dst_ref=sums.at[k],
            send_sem=sum_send.at[k],
            recv_sem=sum_recv.at[k],
            device_id={"gy": flat // nx, "gx": lax.rem(flat, nx)},
            device_id_type=MESH,
        )

    def spread(ref, index, flags):
        for k in range(nb + 2):
            ref[index + (slice(8 * k, 8 * k + 8),)] = jnp.broadcast_to(flags[k : k + 1], (8, lanes))

    def spread_tissue():
        lane = lane_of(8)
        spot = lane % 16
        inner = jnp.logical_and(lane > 0, lane < lanes - 1)
        valid = jnp.logical_or(
            jnp.logical_and(spot >= 1, spot <= 9), jnp.logical_and(spot >= 12, spot <= 14)
        )
        patterns = {}
        for zb in range(blocks_z):
            first = zb * blocks_y
            wide_tiss[zb, 1 : 1 + blocks_y, lanes : lanes + cols] = own_tiss[first : first + blocks_y]
            wide_tiss[zb, 1 : 1 + blocks_y, 0:lanes] = near_tiss[2, first : first + blocks_y, cols - lanes : cols]
            wide_tiss[zb, 1 : 1 + blocks_y, lanes + cols :] = near_tiss[3, first : first + blocks_y, 0:lanes]
            for row, source, at in ((0, (0, 4, 5), first + blocks_y - 1), (1 + blocks_y, (1, 6, 7), first)):
                mid_d, left_d, right_d = source
                wide_tiss[zb, row : row + 1, lanes : lanes + cols] = near_tiss[mid_d, at : at + 1, :]
                wide_tiss[zb, row : row + 1, 0:lanes] = near_tiss[left_d, at : at + 1, cols - lanes : cols]
                wide_tiss[zb, row : row + 1, lanes + cols :] = near_tiss[right_d, at : at + 1, 0:lanes]
            for ci in range(2):
                c = 8 * ci
                for t in range(2):
                    off = lanes + step * t + c
                    flags = (wide_tiss[zb, 0:8, off : off + lanes] - 1.0) * BIG
                    if ci == 0:
                        flags = jnp.where(inner, flags, -BIG)
                    spread(pens, (ci, t, zb), flags)
                left = wide_tiss[zb, 0:8, lanes - 9 + c : 2 * lanes - 9 + c]
                off = lanes + 2 * step + c - 11
                right = wide_tiss[zb, 0:8, off : off + lanes]
                part = jnp.where(lane < 11, left, jnp.where(lane < 16, right, 0.0))
                for shift in (16, 32, 64):
                    part = part + roll(part, shift)
                patterns[zb, ci] = (part - 1.0) * BIG
        low = lane < lanes // 2
        both = [jnp.where(low, patterns[0, ci], patterns[1, ci]) for ci in range(2)]
        own = jnp.where(valid, both[0], -BIG)
        spread(ppens, (0,), own)
        spread(ppens, (1,), both[1])
        spread(ppens, (2,), jnp.where(low, own, -BIG))
        spread(ppens, (3,), patterns[1, 0])
        spread(ppens, (4,), patterns[1, 1])
        spread(ppens, (5,), jnp.where(low, -BIG, own))
        spread(ppens, (6,), patterns[0, 1])

    def shifted(n0, n1, extra):
        lane = lane_of(n0.shape[0])
        return (
            n0,
            jnp.where(lane < 2, roll(n0, 2), roll(n1, 2)),
            jnp.where(lane < lanes - 8, roll(n0, -8), roll(n1, -8)),
            roll(n1, -6) if extra is None else jnp.where(lane < lanes - 6, roll(n1, -6), extra),
        )

    def fill_own(src):
        for z in range(depth):
            four = shifted(src[z, :, 0:lanes], src[z, :, lanes : 2 * lanes], None)
            for k, part in enumerate(four):
                vals[k // 2, k % 2, z, PAD : PAD + rows] = part

    def fill_halo(it):
        lane = lane_of(rows)
        for z in range(depth):
            extra = roll(pack_in[it, 1], lanes - 6 - 16 * z)
            vals[1, 1, z, PAD : PAD + rows] = jnp.where(
                lane < lanes - 6, vals[1, 1, z, PAD : PAD + rows], extra
            )
        plane = lax.broadcasted_iota(jnp.int32, (depth, lanes), 0)
        for d, corner, at, single, alone in (
            (0, 1, 8, 7, PAD - 9), (1, 3, 0, 8, PAD + rows + 8)
        ):
            start = PAD - 8 if d == 0 else PAD + rows
            for z in range(depth):
                extra = roll(corner_in[it, corner, at : at + 8], lanes - 6 - 16 * z)
                four = shifted(rows_in[it, d, z, :, 0:lanes], rows_in[it, d, z, :, lanes : 2 * lanes], extra)
                for k, part in enumerate(four):
                    vals[k // 2, k % 2, z, start : start + 8] = part
            line = jnp.broadcast_to(corner_in[it, corner, single : single + 1], (depth, lanes))
            extra = jnp.zeros((depth, lanes), jnp.float32)
            for z in range(depth):
                extra = jnp.where(plane == z, roll(line, lanes - 6 - 16 * z), extra)
            four = shifted(row_in[it, d, :, 0:lanes], row_in[it, d, :, lanes : 2 * lanes], extra)
            for k, part in enumerate(four):
                for z in range(depth):
                    vals[k // 2, k % 2, z, alone : alone + 1] = part[z : z + 1]
        for start, right_of_left, left, right, left_of_right in (
            (0, corner_in[it, 0], side_in[it, 0, 1], side_in[it, 0, 0], corner_in[it, 1]),
            (PAD, pack_in[it, 0], pack_out[it, 1], pack_out[it, 0], pack_in[it, 1]),
            (PAD + rows, corner_in[it, 2], side_in[it, 1, 1], side_in[it, 1, 0], corner_in[it, 3]),
        ):
            size = left.shape[0]
            lane = lane_of(size)
            spot, group = lane % 16, lane // 16
            zero = jnp.where(
                spot < 9,
                right_of_left,
                jnp.where(
                    spot < 11, roll(left, 9), jnp.where(spot < 15, roll(right, 6), roll(left_of_right, 15))
                ),
            )
            eight = jnp.where(
                spot < 1, roll(right_of_left, -8), jnp.where(spot < 11, roll(left, 1), roll(left_of_right, 7))
            )
            hole = jnp.logical_and(group >= 4, group < 7)
            at = slice(start, start + size)
            packs[0, at] = zero
            packs[1, at] = eight
            packs[2, at] = jnp.where(group == 7, 0.0, zero)
            packs[3, at] = jnp.where(hole, 0.0, roll(zero, 64))
            packs[4, at] = jnp.where(hole, 0.0, roll(eight, 64))
            gap = jnp.logical_and(group >= 1, group < 4)
            packs[5, at] = jnp.where(group == 0, 0.0, zero)
            packs[6, at] = jnp.where(gap, 0.0, roll(eight, 64))
        for t in range(2):
            for ci in range(2):
                for k in range(2):
                    plane = vals[ci, t, depth // 2 - 1 + k]
                    squares[k, ci, t] = plane * plane

    def extent(b):
        k0 = -1 if b > 0 else 0
        k1 = nb + 1 if b < 0 else nb
        return k0, k1, PAD + 8 * (k0 - 1), 8 * (k1 - k0 + 2)

    def add(ref, index, value, init):
        ref[index] = value if init else ref[index] + value

    def weigh(slot, cube, penalty, differ, scale):
        size = cube.shape[0]
        cubes[slot, 0:size] = cube
        inner = size - 16
        total = cube[8 : 8 + inner] + cubes[slot, 7 : 7 + inner] + cubes[slot, 9 : 9 + inner]
        total = total + roll(total, 1) + roll(total, -1)
        weight = jnp.exp2(penalty - total * scale[0:inner])
        return weight, weight * differ[8 : 8 + inner]

    def main_offset(t, offset, init, scale, slot):
        a, b, c = offset
        ci, bb = c // 8, b // 8
        k0, k1, lo, size = extent(b)
        low, planes = max(0, -a), depth - abs(a)
        own_at, far_at = slice(lo, lo + size), slice(lo + b, lo + b + size)

        def differ(z):
            return vals[ci, t, z + a, far_at] - vals[0, t, z, own_at]

        def outside(z):
            if a == 0:
                return None
            if (z < low) == (a > 0):
                return squares[0 if a > 0 else 1, ci, t, far_at]
            return squares[1 if a > 0 else 0, 0, t, own_at]

        own_pen, far_pen = slice(8 * (k0 + 1), 8 * (k1 + 1)), slice(8 * (k0 + bb + 1), 8 * (k1 + bb + 1))
        po, qo = -8 * k0, -8 * (bb + k0)
        penalty = None
        high = low + planes
        before = outside(low - 1)
        diffs = {low: differ(low)}
        sqs = {low: diffs[low] * diffs[low]}
        for z in range(low, high, 2):
            zb = z // 4
            if z % 4 == 0:
                penalty = pens[0, t, zb, own_pen] + pens[ci, t, (z + a) // 4, far_pen]
            diffs[z + 1] = differ(z + 1)
            sqs[z + 1] = diffs[z + 1] * diffs[z + 1]
            pair = sqs[z] + sqs[z + 1]
            if z + 2 < high:
                diffs[z + 2] = differ(z + 2)
                sqs[z + 2] = diffs[z + 2] * diffs[z + 2]
                after = sqs[z + 2]
            else:
                after = outside(high)
            for plane, cube in (
                (z, pair if before is None else pair + before),
                (z + 1, pair if after is None else pair + after),
            ):
                weight, push = weigh(slot % SLOTS, cube, penalty, diffs[plane], scale)
                slot += 1
                add(acc, (0, 0, t, plane), push[po : po + rows], init)
                add(acc, (0, 1, t, plane), weight[po : po + rows], init)
                far = plane + a
                add(acc, (ci, 0, t, far), -push[qo : qo + rows] if init else -push[qo : qo + rows], init)
                add(acc, (ci, 1, t, far), weight[qo : qo + rows], init)
            before = sqs[z + 1]
        return slot

    def pack_offset(offset, init, scale, slot):
        a, b, c = offset
        ci, bb = c // 8, b // 8
        k0, k1, lo, size = extent(b)
        near, far = {0: (0, ci), 4: (2, 3 + ci), -4: (5, 6)}[a]
        differ = packs[far, lo + b : lo + b + size] - packs[near, lo : lo + size]
        square = differ * differ
        up, down = roll(square, 16), roll(square, -16)
        if a == 0:
            lane = lane_of(size)
            up = jnp.where(lane >= 16, up, 0.0)
            down = jnp.where(lane < lanes - 16, down, 0.0)
        penalty = ppens[near, 8 * (k0 + 1) : 8 * (k1 + 1)] + ppens[far, 8 * (k0 + bb + 1) : 8 * (k1 + bb + 1)]
        weight, push = weigh(slot, square + up + down, penalty, differ, scale)
        po, qo = -8 * k0, -8 * (bb + k0)
        key = ci + 2 * (a != 0)
        first_p, first_q = init
        add(pacc, (0, 0), push[po : po + rows], first_p)
        add(pacc, (0, 1), weight[po : po + rows], first_p)
        add(pacc, (key, 0), -push[qo : qo + rows], first_q)
        add(pacc, (key, 1), weight[qo : qo + rows], first_q)

    def gather(scale):
        def body(t, carry):
            slot = 0
            for k, offset in enumerate(LEVEL + CROSS):
                slot = main_offset(t, offset, k == 0, scale, slot)
            return carry

        lax.fori_loop(0, 2, body, 0)
        seen = set()
        for k, offset in enumerate(LEVEL + CROSS):
            key = (offset[0] != 0, offset[2])
            fresh = key not in seen and key != (False, 0)
            seen.add(key)
            pack_offset(offset, (k == 0, fresh), scale, k % SLOTS)

    def finish(src, dst):
        lane = lane_of(rows)
        spot = lane % 16
        merged = []
        for kind in range(2):
            zero = pacc[0, kind] + roll(pacc[2, kind], 64)
            eight = pacc[1, kind] + roll(pacc[3, kind], 64)
            eight = eight + jnp.where(spot == 1, roll(zero, -8), 0.0)
            merged.append(
                jnp.where(jnp.logical_or(spot >= 14, spot == 0), roll(zero, -14), jnp.where(spot < 10, eight, 0.0))
            )
        for z in range(depth):
            sides = []
            for kind in range(2):
                near = roll(merged[kind], -(16 * z + 1))
                first = acc[0, kind, 0, z]
                second = roll(acc[0, kind, 1, z], -2)
                far_first = roll(acc[1, kind, 0, z], 8)
                far_second = roll(acc[1, kind, 1, z], 6)
                sides.append((
                    first + jnp.where(lane < 9, near, far_first) + jnp.where(lane == lanes - 1, second, 0.0),
                    jnp.where(lane >= lanes - 3, near, second) + jnp.where(lane < 7, far_first, far_second),
                ))
            for t in range(2):
                at = slice(t * lanes, (t + 1) * lanes)
                dst[z, :, at] = src[z, :, at] + sides[0][t] / (sides[1][t] + 1.0)

    loads[0].wait()
    widen = (
        lax.broadcasted_iota(jnp.int32, (blocks_x, cols), 1) // 8
        == lax.broadcasted_iota(jnp.int32, (blocks_x, cols), 0)
    ).astype(jnp.float32)
    for zb in range(blocks_z):
        flags = mask_ref[zb].astype(jnp.float32)
        own_tiss[zb * blocks_y : (zb + 1) * blocks_y] = jnp.dot(
            flags, widen, preferred_element_type=jnp.float32
        )
    loads[1].wait()
    total = jnp.zeros((8, cols), jnp.float32)
    count = jnp.zeros((8, cols), jnp.float32)
    for z in range(1, depth - 1):
        residual = vol_ref[z] - 0.5 * (vol_ref[z - 1] + vol_ref[z + 1])
        for yb in range(blocks_y):
            line = (z // 4) * blocks_y + yb
            flag = jnp.broadcast_to(own_tiss[line : line + 1], (8, cols))
            piece = residual[8 * yb : 8 * yb + 8]
            total = total + flag * piece * piece
            count = count + flag
    total = jnp.sum(total, axis=0, keepdims=True)
    count = jnp.sum(count, axis=0, keepdims=True)
    tiles = cols // lanes
    total = functools.reduce(jnp.add, [total[:, i * lanes : (i + 1) * lanes] for i in range(tiles)])
    count = functools.reduce(jnp.add, [count[:, i * lanes : (i + 1) * lanes] for i in range(tiles)])
    lane = lax.broadcasted_iota(jnp.int32, (1, lanes), 1)
    sums[0] = jnp.where(
        lane < lanes // 2,
        jnp.sum(total, axis=1, keepdims=True),
        jnp.sum(count, axis=1, keepdims=True),
    )
    make_packs(vol_ref, 0)
    pl.semaphore_wait(barrier, peers - 1)
    for k in range(1, peers):
        sum_copy(k).start()
    start_halo(vol_ref, 0)
    for it in range(ITERS):
        clear_missing(it)
    fill_own(vol_ref)
    wait_halo(vol_ref, 0)
    spread_tissue()
    fill_halo(0)
    for k in range(1, peers):
        sum_copy(k).wait_recv()
    everything = sums[0]
    for k in range(1, peers):
        everything = everything + sums[k]
    summed = everything[:, 0:1] * (2.0 / 3.0)
    tissue_count = everything[:, lanes // 2 : lanes // 2 + 1]
    variance = summed / jnp.maximum(tissue_count, 1.0) + 1e-05
    width = 54.0 * smooth_ref[0] * smooth_ref[0]
    scale = jnp.broadcast_to(LOG2E / (width * variance), (rows + 8, lanes))
    gather(scale)
    finish(vol_ref, mid)
    make_packs(mid, 1)
    start_halo(mid, 1)
    fill_own(mid)
    wait_halo(mid, 1)
    fill_halo(1)
    gather(scale)
    finish(mid, out_ref)
    wait_sent(vol_ref, 0)
    wait_sent(mid, 1)
    for k in range(1, peers):
        sum_copy(k).wait_send()


def on_device(volume, tissue_mask, smoothing):
    ny, nx = lax.axis_size("gy"), lax.axis_size("gx")
    depth, rows, cols = volume.shape
    blocks_z, blocks_y, blocks_x = tissue_mask.shape
    lanes = 128
    assert depth == 8 and cols == 2 * lanes and blocks_z == 2
    flag_rows = -(-(blocks_y + 2) // 8) * 8
    f32 = jnp.float32
    vmem = pl.BlockSpec(memory_space=pltpu.VMEM)
    anywhere = pl.BlockSpec(memory_space=pltpu.HBM)
    return pl.pallas_call(
        functools.partial(kernel, ny, nx),
        out_shape=jax.ShapeDtypeStruct(volume.shape, f32),
        in_specs=[pl.BlockSpec(memory_space=pltpu.SMEM), anywhere, anywhere],
        out_specs=vmem,
        scratch_shapes=[
            pltpu.VMEM((depth, rows, cols), f32),
            pltpu.VMEM((blocks_z, blocks_y, blocks_x), jnp.int32),
            pltpu.VMEM((depth, rows, cols), f32),
            pltpu.VMEM((2, 2, depth, rows + 2 * PAD, lanes), f32),
            pltpu.VMEM((7, rows + 2 * PAD, lanes), f32),
            pltpu.VMEM((2, 2, 2, rows + 2 * PAD, lanes), f32),
            pltpu.VMEM((SLOTS, rows + 24, lanes), f32),
            pltpu.VMEM((2, 2, 2, depth, rows, lanes), f32),
            pltpu.VMEM((4, 2, rows, lanes), f32),
            pltpu.VMEM((2, 2, blocks_z, rows + 16, lanes), f32),
            pltpu.VMEM((7, rows + 16, lanes), f32),
            pltpu.VMEM((blocks_z * blocks_y, cols), f32),
            pltpu.VMEM((len(DIRS), blocks_z * blocks_y, cols), f32),
            pltpu.VMEM((blocks_z, flag_rows, cols + 2 * lanes), f32),
            pltpu.VMEM((ITERS, 2, depth, 8, cols), f32),
            pltpu.VMEM((ITERS, 2, depth, cols), f32),
            pltpu.VMEM((ITERS, 2, depth, cols), f32),
            pltpu.VMEM((ITERS, 2, rows, lanes), f32),
            pltpu.VMEM((ITERS, 2, rows, lanes), f32),
            pltpu.VMEM((ITERS, 2, 2, 16, lanes), f32),
            pltpu.VMEM((ITERS, 4, 16, lanes), f32),
            pltpu.VMEM((ny * nx, 1, lanes), f32),
            pltpu.SemaphoreType.DMA((2,)),
            pltpu.SemaphoreType.DMA((ny * nx,)),
            pltpu.SemaphoreType.DMA((ny * nx,)),
            pltpu.SemaphoreType.DMA((ITERS, len(DIRS), 4)),
            pltpu.SemaphoreType.DMA((ITERS, len(DIRS), 4)),
        ],
        compiler_params=pltpu.CompilerParams(
            collective_id=0, has_side_effects=True, vmem_limit_bytes=16 * 2**20
        ),
    )(
        smoothing,
        pltpu.with_memory_space_constraint(volume, pltpu.HBM),
        pltpu.with_memory_space_constraint(tissue_mask, pltpu.HBM),
    )


def solution(mesh):
    placed = (P(None, ("slab", "gy"), "gx"), P(None, ("slab", "gy"), "gx"), P())
    return jax.shard_map(
        on_device,
        mesh=mesh,
        in_specs=placed,
        out_specs=P(None, ("slab", "gy"), "gx"),
        check_vma=False,
    )
```

time: 29.6 us -> 26.9 us (0.909)
  Pallas kernels: 28 us -> 25.3 us
    pallas_call x1, Pallas kernels: 28 us -> 25.3 us  [on_device(): pl.pallas_call(functools.partial(kernel, ny, nx), out_shape=jax.ShapeDtyp...]
where the time goes in v1:
time: 26.9 us; the launch traced here: 26.7 us
  Pallas kernels  25.3 us (94%)
  local copies, waits for them, and re-layouts  0.71 us (3%)
  between operations  0.66 us (2%)
    pallas_call x1, Pallas kernels, on_device(): pl.pallas_call(functools.partial(kernel, ny, nx), out_shape=jax.ShapeDtyp...  25.3 us
    unnamed x1, local copies, waits for them, and re-layouts  0.71 us

profile of v1, /device:TPU:0, one launch (start us, length us, event | category | flops | bytes accessed | tf_op | source)
XLA Modules:
  0.0 26.7 jit_solution(9919147011882013680)
XLA Ops:
  0.7 25.3 %shard_map.37 = f32[8,32,256]{2,1,0:T(8,128)S(1)} custom-call(f32[1]{0:T(128)S(6)} %copy.5.smooth_ref, f32[8,32,256]{2,1,0:T(8,128)} %vol_hbm.1, s32[2,4,32]{2,1,0:T(4,128)} %mask_hbm.1), custom_call_target="tpu_custom_call" | custom-call | tf_op jit(solution)/shard_map/pallas_call | solution.py:492
  26.0 0.7 %copy.6 = f32[8,32,256]{2,1,0:T(8,128)} copy(f32[8,32,256]{2,1,0:T(8,128)S(1)} %shard_map.37) | data formatting | bytes 524288

commit v2 on v1

--- a/solution.py
+++ b/solution.py
@@ -22,25 +22,49 @@
 
 def kernel(
     ny, nx, smooth_ref, vol_hbm, mask_hbm, out_ref, vol_ref, mask_ref, mid, vals, packs, squares,
-    cubes, acc, pacc, pens, ppens, own_tiss, near_tiss, wide_tiss,
-    rows_in, row_in, row_out, pack_out, pack_in, side_in, corner_in, sums,
-    load_sem, sum_send, sum_recv, halo_send, halo_recv,
+    cubes, totals, band, acc, pcubes, found, pens, ppens, own_tiss, near_tiss, wide_tiss,
+    rows_in, row_in, row_out, pack_out, pack_in, corner_in, row_sums, col_sums,
+    load_sem, known, sum_send, sum_recv, halo_send, halo_recv,
 ):
     depth, rows, cols = vol_ref.shape
     lanes = 128
     blocks_z, blocks_y, blocks_x = mask_ref.shape
     nb = rows // 8
     step = lanes - 2
-    peers = ny * nx
     gy, gx = lax.axis_index("gy"), lax.axis_index("gx")
-    me = gy * nx + gx
 
     barrier = pltpu.get_barrier_semaphore()
-    for k in range(1, peers):
-        flat = lax.rem(me + k, peers)
-        pl.semaphore_signal(
-            barrier, inc=1, device_id={"gy": flat // nx, "gx": lax.rem(flat, nx)}, device_id_type=MESH
-        )
+
+    def exists(dy, dx):
+        found = None
+        for move, pos, count in ((dy, gy, ny), (dx, gx, nx)):
+            if move == 0:
+                continue
+            here = pos < count - move if move > 0 else pos >= -move
+            found = here if found is None else jnp.logical_and(found, here)
+        return found
+
+    def peer(axis, k):
+        pos, count = (gy, ny) if axis == "gy" else (gx, nx)
+        return {axis: jnp.where(pos + k >= count, pos + k - count, pos + k)}
+
+    def greet(semaphore, moves):
+        for dy, dx in moves:
+
+            @pl.when(exists(dy, dx))
+            def _():
+                pl.semaphore_signal(
+                    semaphore, inc=1, device_id={"gy": gy + dy, "gx": gx + dx}, device_id_type=MESH
+                )
+
+    def present(moves):
+        return functools.reduce(jnp.add, [exists(dy, dx).astype(jnp.int32) for dy, dx in moves])
+
+    column = [(dy, 0) for dy in (1, -1, 2, -2)]
+    others = column + list(DIRS[4:])
+    for k in range(1, nx):
+        pl.semaphore_signal(barrier, inc=1, device_id=peer("gx", k), device_id_type=MESH)
+    greet(barrier, others)
 
     loads = [
         pltpu.make_async_copy(mask_hbm, mask_ref, load_sem.at[0]),
@@ -52,28 +76,23 @@
     def lane_of(n):
         return lax.broadcasted_iota(jnp.int32, (n, lanes), 1)
 
-    def exists(dy, dx):
-        found = None
-        for move, pos, count in ((dy, gy, ny), (dx, gx, nx)):
-            if move == 0:
-                continue
-            here = pos < count - 1 if move > 0 else pos > 0
-            found = here if found is None else jnp.logical_and(found, here)
-        return found
-
     def roll(x, shift):
         shift = shift % lanes
         return pltpu.roll(x, shift, 1) if shift else x
 
+    def packed(planes):
+        group = lane_of(planes[0].shape[0]) // 16
+        left, right = planes[0][:, 0:lanes], roll(planes[0][:, cols - lanes : cols], 9)
+        for z in range(1, depth):
+            right = jnp.where(group == z, roll(planes[z][:, cols - lanes : cols], 16 * z + 9), right)
+            left = jnp.where(group == z, roll(planes[z][:, 0:lanes], 16 * z), left)
+        return left, right
+
     def make_packs(src, it):
-        group = lane_of(rows) // 16
-        right = jnp.zeros((rows, lanes), jnp.float32)
-        left = right
         for z in range(depth):
-            right = jnp.where(group == z, roll(src[z, :, cols - lanes : cols], 16 * z + 9), right)
-            left = jnp.where(group == z, roll(src[z, :, 0:lanes], 16 * z), left)
             row_out[it, 0, z : z + 1] = src[z, rows - 9 : rows - 8, :]
             row_out[it, 1, z : z + 1] = src[z, 8:9, :]
+        left, right = packed([src[z] for z in range(depth)])
         pack_out[it, 0] = right
         pack_out[it, 1] = left
 
@@ -84,8 +103,6 @@
             start = rows - 8 if dy > 0 else 0
             pairs.append((src.at[:, start : start + 8, :], rows_in.at[it, d]))
             pairs.append((row_out.at[it, d], row_in.at[it, d]))
-            start = rows - 16 if dy > 0 else 0
-            pairs.append((pack_out.at[it, :, start : start + 16], side_in.at[it, d]))
         elif dy == 0:
             pairs.append((pack_out.at[it, d - 2], pack_in.at[it, d - 2]))
         else:
@@ -114,7 +131,6 @@
                 if dx == 0:
                     rows_in[it, d] = jnp.zeros(rows_in.shape[2:], jnp.float32)
                     row_in[it, d] = jnp.zeros(row_in.shape[2:], jnp.float32)
-                    side_in[it, d] = jnp.zeros(side_in.shape[2:], jnp.float32)
                 elif dy == 0:
                     pack_in[it, d - 2] = jnp.zeros(pack_in.shape[2:], jnp.float32)
                 else:
@@ -146,16 +162,20 @@
                 for copy in copies(src, it, d):
                     copy.wait_send()
 
-    def sum_copy(k):
-        flat = lax.rem(me + k, peers)
-        return pltpu.make_async_remote_copy(
-            src_ref=sums.at[0],
-            dst_ref=sums.at[k],
-            send_sem=sum_send.at[k],
-            recv_sem=sum_recv.at[k],
-            device_id={"gy": flat // nx, "gx": lax.rem(flat, nx)},
-            device_id_type=MESH,
-        )
+    def sum_copies(axis):
+        count, buffer = (nx, row_sums) if axis == "gx" else (ny, col_sums)
+        stage = 0 if axis == "gx" else 1
+        return [
+            pltpu.make_async_remote_copy(
+                src_ref=buffer.at[0],
+                dst_ref=buffer.at[k],
+                send_sem=sum_send.at[stage, k],
+                recv_sem=sum_recv.at[stage, k],
+                device_id=peer(axis, k),
+                device_id_type=MESH,
+            )
+            for k in range(1, count)
+        ]
 
     def spread(ref, index, flags):
         for k in range(nb + 2):
@@ -204,6 +224,7 @@
         spread(ppens, (4,), patterns[1, 1])
         spread(ppens, (5,), jnp.where(low, -BIG, own))
         spread(ppens, (6,), patterns[0, 1])
+        spread(ppens, (7,), patterns[0, 0])
 
     def shifted(n0, n1, extra):
         lane = lane_of(n0.shape[0])
@@ -245,11 +266,16 @@
             for k, part in enumerate(four):
                 for z in range(depth):
                     vals[k // 2, k % 2, z, alone : alone + 1] = part[z : z + 1]
-        for start, right_of_left, left, right, left_of_right in (
-            (0, corner_in[it, 0], side_in[it, 0, 1], side_in[it, 0, 0], corner_in[it, 1]),
-            (PAD, pack_in[it, 0], pack_out[it, 1], pack_out[it, 0], pack_in[it, 1]),
-            (PAD + rows, corner_in[it, 2], side_in[it, 1, 1], side_in[it, 1, 0], corner_in[it, 3]),
-        ):
+        parts = [(PAD, pack_in[it, 0], (pack_out[it, 1], pack_out[it, 0]), pack_in[it, 1])]
+        for d, at, single in ((0, 8, 7), (1, 0, 8)):
+            before, after = corner_in[it, 2 * d], corner_in[it, 2 * d + 1]
+            start = PAD - 8 if d == 0 else PAD + rows
+            alone = PAD - 9 if d == 0 else PAD + rows + 8
+            near = packed([rows_in[it, d, z] for z in range(depth)])
+            line = packed([row_in[it, d, z : z + 1] for z in range(depth)])
+            parts.append((start, before[at : at + 8], near, after[at : at + 8]))
+            parts.append((alone, before[single : single + 1], line, after[single : single + 1]))
+        for start, right_of_left, (left, right), left_of_right in parts:
             size = left.shape[0]
             lane = lane_of(size)
             spot, group = lane % 16, lane // 16
@@ -273,6 +299,7 @@
             gap = jnp.logical_and(group >= 1, group < 4)
             packs[5, at] = jnp.where(group == 0, 0.0, zero)
             packs[6, at] = jnp.where(gap, 0.0, roll(eight, 64))
+            packs[7, at] = jnp.where(gap, 0.0, roll(zero, 64))
         for t in range(2):
             for ci in range(2):
                 for k in range(2):
@@ -287,110 +314,153 @@
     def add(ref, index, value, init):
         ref[index] = value if init else ref[index] + value
 
-    def weigh(slot, cube, penalty, differ, scale):
-        size = cube.shape[0]
-        cubes[slot, 0:size] = cube
-        inner = size - 16
-        total = cube[8 : 8 + inner] + cubes[slot, 7 : 7 + inner] + cubes[slot, 9 : 9 + inner]
-        total = total + roll(total, 1) + roll(total, -1)
-        weight = jnp.exp2(penalty - total * scale[0:inner])
-        return weight, weight * differ[8 : 8 + inner]
-
-    def main_offset(t, offset, init, scale, slot):
+    def box(parts):
+        tops = [part.astype(jnp.bfloat16).astype(jnp.float32) for part in parts]
+        lhs = [jnp.concatenate([top, part - top], axis=1) for part, top in zip(parts, tops)]
+        return jnp.dot(jnp.concatenate(lhs, axis=0), band[...], preferred_element_type=jnp.float32)
+
+    def main_offset(t, offset, init, scale, slot, mode):
         a, b, c = offset
         ci, bb = c // 8, b // 8
         k0, k1, lo, size = extent(b)
+        inner = size - 16
         low, planes = max(0, -a), depth - abs(a)
-        own_at, far_at = slice(lo, lo + size), slice(lo + b, lo + b + size)
-
-        def differ(z):
-            return vals[ci, t, z + a, far_at] - vals[0, t, z, own_at]
+        high = low + planes
+
+        def differ(z, low_row, count):
+            far = slice(low_row + b, low_row + b + count)
+            return vals[ci, t, z + a, far] - vals[0, t, z, low_row : low_row + count]
 
         def outside(z):
             if a == 0:
                 return None
             if (z < low) == (a > 0):
-                return squares[0 if a > 0 else 1, ci, t, far_at]
-            return squares[1 if a > 0 else 0, 0, t, own_at]
+                return squares[0 if a > 0 else 1, ci, t, lo + b : lo + b + size]
+            return squares[1 if a > 0 else 0, 0, t, lo : lo + size]
 
         own_pen, far_pen = slice(8 * (k0 + 1), 8 * (k1 + 1)), slice(8 * (k0 + bb + 1), 8 * (k1 + bb + 1))
         po, qo = -8 * k0, -8 * (bb + k0)
         penalty = None
-        high = low + planes
-        before = outside(low - 1)
-        diffs = {low: differ(low)}
-        sqs = {low: diffs[low] * diffs[low]}
+        before = None
+        diffs, sqs = {}, {}
+        queue = []
+
+        def grow(z):
+            diffs[z] = differ(z, lo, size)
+            sqs[z] = diffs[z] * diffs[z]
+
+        if mode != "apply":
+            before = outside(low - 1)
+            grow(low)
         for z in range(low, high, 2):
-            zb = z // 4
-            if z % 4 == 0:
-                penalty = pens[0, t, zb, own_pen] + pens[ci, t, (z + a) // 4, far_pen]
-            diffs[z + 1] = differ(z + 1)
-            sqs[z + 1] = diffs[z + 1] * diffs[z + 1]
-            pair = sqs[z] + sqs[z + 1]
-            if z + 2 < high:
-                diffs[z + 2] = differ(z + 2)
-                sqs[z + 2] = diffs[z + 2] * diffs[z + 2]
-                after = sqs[z + 2]
-            else:
-                after = outside(high)
-            for plane, cube in (
-                (z, pair if before is None else pair + before),
-                (z + 1, pair if after is None else pair + after),
-            ):
-                weight, push = weigh(slot % SLOTS, cube, penalty, diffs[plane], scale)
+            if z % 4 == 0 and mode != "measure":
+                penalty = pens[0, t, z // 4, own_pen] + pens[ci, t, (z + a) // 4, far_pen]
+            cubed = (None, None)
+            if mode != "apply":
+                grow(z + 1)
+                pair = sqs[z] + sqs[z + 1]
+                if z + 2 < high:
+                    grow(z + 2)
+                    after = sqs[z + 2]
+                else:
+                    after = outside(high)
+                cubed = (
+                    pair if before is None else pair + before,
+                    pair if after is None else pair + after,
+                )
+                before = sqs[z + 1]
+            for plane, cube in zip((z, z + 1), cubed):
+                if mode != "apply":
+                    at = slot % SLOTS
+                    cubes[at, 0:size] = cube
+                    total = cube[8 : 8 + inner] + cubes[at, 7 : 7 + inner] + cubes[at, 9 : 9 + inner]
+                    if mode == "measure":
+                        slot += 1
+                        queue.append(total)
+                        continue
+                    total = total + roll(total, 1) + roll(total, -1)
+                if mode == "apply":
+                    total = totals[t, slot, 0:inner]
+                    gap = differ(plane, lo + 8, inner)
+                else:
+                    gap = diffs[plane][8 : 8 + inner]
                 slot += 1
+                weight = jnp.exp2(penalty - total * scale[0:inner])
+                push = weight * gap
                 add(acc, (0, 0, t, plane), push[po : po + rows], init)
                 add(acc, (0, 1, t, plane), weight[po : po + rows], init)
                 far = plane + a
-                add(acc, (ci, 0, t, far), -push[qo : qo + rows] if init else -push[qo : qo + rows], init)
+                if init:
+                    acc[ci, 0, t, far] = -push[qo : qo + rows]
+                else:
+                    acc[ci, 0, t, far] -= push[qo : qo + rows]
                 add(acc, (ci, 1, t, far), weight[qo : qo + rows], init)
-            before = sqs[z + 1]
+        if mode == "measure":
+            summed = box(queue)
+            for k in range(len(queue)):
+                totals[t, slot - len(queue) + k, 0:inner] = summed[k * inner : (k + 1) * inner]
         return slot
 
-    def pack_offset(offset, init, scale, slot):
-        a, b, c = offset
-        ci, bb = c // 8, b // 8
-        k0, k1, lo, size = extent(b)
-        near, far = {0: (0, ci), 4: (2, 3 + ci), -4: (5, 6)}[a]
-        differ = packs[far, lo + b : lo + b + size] - packs[near, lo : lo + size]
-        square = differ * differ
-        up, down = roll(square, 16), roll(square, -16)
-        if a == 0:
-            lane = lane_of(size)
-            up = jnp.where(lane >= 16, up, 0.0)
-            down = jnp.where(lane < lanes - 16, down, 0.0)
-        penalty = ppens[near, 8 * (k0 + 1) : 8 * (k1 + 1)] + ppens[far, 8 * (k0 + bb + 1) : 8 * (k1 + bb + 1)]
-        weight, push = weigh(slot, square + up + down, penalty, differ, scale)
-        po, qo = -8 * k0, -8 * (bb + k0)
-        key = ci + 2 * (a != 0)
-        first_p, first_q = init
-        add(pacc, (0, 0), push[po : po + rows], first_p)
-        add(pacc, (0, 1), weight[po : po + rows], first_p)
-        add(pacc, (key, 0), -push[qo : qo + rows], first_q)
-        add(pacc, (key, 1), weight[qo : qo + rows], first_q)
-
-    def gather(scale):
-        def body(t, carry):
-            slot = 0
-            for k, offset in enumerate(LEVEL + CROSS):
-                slot = main_offset(t, offset, k == 0, scale, slot)
-            return carry
-
-        lax.fori_loop(0, 2, body, 0)
-        seen = set()
+    def main_gather(t, scale, mode):
+        slot = 0
         for k, offset in enumerate(LEVEL + CROSS):
-            key = (offset[0] != 0, offset[2])
-            fresh = key not in seen and key != (False, 0)
-            seen.add(key)
-            pack_offset(offset, (k == 0, fresh), scale, k % SLOTS)
-
-    def finish(src, dst):
+            slot = main_offset(t, offset, k == 0, scale, slot, mode)
+        return 0
+
+    packed_items = []
+    for a, b, c in LEVEL + CROSS:
+        near, far = {0: (0, c // 8), 4: (2, 3 + c // 8), -4: (5, 6)}[a]
+        packed_items.append((near, far, b, c // 8 + 2 * (a != 0), a == 0))
+
+    def pack_differ(near, far, b, low, size):
+        return packs[far, low + b : low + b + size] - packs[near, low : low + size]
+
+    def pack_measure():
+        for k, (near, far, b, key, masked) in enumerate(packed_items):
+            k0, k1, lo, size = extent(b)
+            gap = pack_differ(near, far, b, lo, size)
+            square = gap * gap
+            up, down = roll(square, 16), roll(square, -16)
+            if masked:
+                lane = lane_of(size)
+                up = jnp.where(lane >= 16, up, 0.0)
+                down = jnp.where(lane < lanes - 16, down, 0.0)
+            pcubes[k, 0:size] = square + up + down
+        for k, (near, far, b, key, masked) in enumerate(packed_items):
+            inner = extent(b)[3] - 16
+            total = pcubes[k, 7 : 7 + inner] + pcubes[k, 8 : 8 + inner] + pcubes[k, 9 : 9 + inner]
+            found[k, 0:inner] = total + roll(total, 1) + roll(total, -1)
+
+    def pack_apply(scale):
+        parts = [[None] * 4, [None] * 4]
+
+        def gain(kind, key, value, minus):
+            old = parts[kind][key]
+            if old is None:
+                parts[kind][key] = -value if minus else value
+            else:
+                parts[kind][key] = old - value if minus else old + value
+
+        for k, (near, far, b, key, masked) in enumerate(packed_items):
+            k0, k1, lo, size = extent(b)
+            bb, inner = b // 8, size - 16
+            penalty = ppens[near, 8 * (k0 + 1) : 8 * (k1 + 1)] + ppens[far, 8 * (k0 + bb + 1) : 8 * (k1 + bb + 1)]
+            weight = jnp.exp2(penalty - found[k, 0:inner] * scale[0:inner])
+            push = weight * pack_differ(near, far, b, lo + 8, inner)
+            po, qo = -8 * k0, -8 * (bb + k0)
+            gain(0, 0, push[po : po + rows], False)
+            gain(1, 0, weight[po : po + rows], False)
+            gain(0, key, push[qo : qo + rows], True)
+            gain(1, key, weight[qo : qo + rows], False)
+        return parts
+
+    def finish(src, dst, parts):
         lane = lane_of(rows)
         spot = lane % 16
         merged = []
         for kind in range(2):
-            zero = pacc[0, kind] + roll(pacc[2, kind], 64)
-            eight = pacc[1, kind] + roll(pacc[3, kind], 64)
+            zero = parts[kind][0] + roll(parts[kind][2], 64)
+            eight = parts[kind][1] + roll(parts[kind][3], 64)
             eight = eight + jnp.where(spot == 1, roll(zero, -8), 0.0)
             merged.append(
                 jnp.where(jnp.logical_or(spot >= 14, spot == 0), roll(zero, -14), jnp.where(spot < 10, eight, 0.0))
@@ -411,6 +481,9 @@
                 at = slice(t * lanes, (t + 1) * lanes)
                 dst[z, :, at] = src[z, :, at] + sides[0][t] / (sides[1][t] + 1.0)
 
+    row_at = lax.broadcasted_iota(jnp.int32, (2 * lanes, lanes), 0) % lanes
+    col_at = lax.broadcasted_iota(jnp.int32, (2 * lanes, lanes), 1)
+    band[...] = (jnp.abs(row_at - col_at) <= 1).astype(jnp.float32)
     loads[0].wait()
     widen = (
         lax.broadcasted_iota(jnp.int32, (blocks_x, cols), 1) // 8
@@ -438,45 +511,58 @@
     total = functools.reduce(jnp.add, [total[:, i * lanes : (i + 1) * lanes] for i in range(tiles)])
     count = functools.reduce(jnp.add, [count[:, i * lanes : (i + 1) * lanes] for i in range(tiles)])
     lane = lax.broadcasted_iota(jnp.int32, (1, lanes), 1)
-    sums[0] = jnp.where(
+    row_sums[0] = jnp.where(
         lane < lanes // 2,
         jnp.sum(total, axis=1, keepdims=True),
         jnp.sum(count, axis=1, keepdims=True),
     )
     make_packs(vol_ref, 0)
-    pl.semaphore_wait(barrier, peers - 1)
-    for k in range(1, peers):
-        sum_copy(k).start()
+    pl.semaphore_wait(barrier, nx - 1 + present(others))
+    rounds = known.shape[0]
+    for copy in sum_copies("gx"):
+        copy.start()
+    greet(known.at[0], column)
     start_halo(vol_ref, 0)
     for it in range(ITERS):
         clear_missing(it)
     fill_own(vol_ref)
+    for k in range(rounds):
+        pl.semaphore_wait(known.at[k], present(column))
+        if k + 1 < rounds:
+            greet(known.at[k + 1], column)
+    for copy in sum_copies("gx"):
+        copy.wait_recv()
+    col_sums[0] = functools.reduce(jnp.add, [row_sums[k] for k in range(nx)])
+    for copy in sum_copies("gy"):
+        copy.start()
     wait_halo(vol_ref, 0)
     spread_tissue()
     fill_halo(0)
-    for k in range(1, peers):
-        sum_copy(k).wait_recv()
-    everything = sums[0]
-    for k in range(1, peers):
-        everything = everything + sums[k]
+    lax.fori_loop(0, 2, lambda t, carry: main_gather(t, None, "measure"), 0)
+    pack_measure()
+    for copy in sum_copies("gy"):
+        copy.wait_recv()
+    everything = functools.reduce(jnp.add, [col_sums[k] for k in range(ny)])
     summed = everything[:, 0:1] * (2.0 / 3.0)
     tissue_count = everything[:, lanes // 2 : lanes // 2 + 1]
     variance = summed / jnp.maximum(tissue_count, 1.0) + 1e-05
     width = 54.0 * smooth_ref[0] * smooth_ref[0]
     scale = jnp.broadcast_to(LOG2E / (width * variance), (rows + 8, lanes))
-    gather(scale)
-    finish(vol_ref, mid)
+    lax.fori_loop(0, 2, lambda t, carry: main_gather(t, scale, "apply"), 0)
+    finish(vol_ref, mid, pack_apply(scale))
     make_packs(mid, 1)
     start_halo(mid, 1)
     fill_own(mid)
     wait_halo(mid, 1)
     fill_halo(1)
-    gather(scale)
-    finish(mid, out_ref)
+    lax.fori_loop(0, 2, lambda t, carry: main_gather(t, scale, "both"), 0)
+    pack_measure()
+    finish(mid, out_ref, pack_apply(scale))
     wait_sent(vol_ref, 0)
     wait_sent(mid, 1)
-    for k in range(1, peers):
-        sum_copy(k).wait_send()
+    for axis in ("gx", "gy"):
+        for copy in sum_copies(axis):
+            copy.wait_send()
 
 
 def on_device(volume, tissue_mask, smoothing):
@@ -499,13 +585,16 @@
             pltpu.VMEM((blocks_z, blocks_y, blocks_x), jnp.int32),
             pltpu.VMEM((depth, rows, cols), f32),
             pltpu.VMEM((2, 2, depth, rows + 2 * PAD, lanes), f32),
-            pltpu.VMEM((7, rows + 2 * PAD, lanes), f32),
+            pltpu.VMEM((8, rows + 2 * PAD, lanes), f32),
             pltpu.VMEM((2, 2, 2, rows + 2 * PAD, lanes), f32),
             pltpu.VMEM((SLOTS, rows + 24, lanes), f32),
+            pltpu.VMEM((2, len(LEVEL) * depth + len(CROSS) * depth // 2, rows + 8, lanes), f32),
+            pltpu.VMEM((2 * lanes, lanes), f32),
             pltpu.VMEM((2, 2, 2, depth, rows, lanes), f32),
-            pltpu.VMEM((4, 2, rows, lanes), f32),
+            pltpu.VMEM((13, rows + 24, lanes), f32),
+            pltpu.VMEM((13, rows + 8, lanes), f32),
             pltpu.VMEM((2, 2, blocks_z, rows + 16, lanes), f32),
-            pltpu.VMEM((7, rows + 16, lanes), f32),
+            pltpu.VMEM((8, rows + 16, lanes), f32),
             pltpu.VMEM((blocks_z * blocks_y, cols), f32),
             pltpu.VMEM((len(DIRS), blocks_z * blocks_y, cols), f32),
             pltpu.VMEM((blocks_z, flag_rows, cols + 2 * lanes), f32),
@@ -514,14 +603,15 @@
             pltpu.VMEM((ITERS, 2, depth, cols), f32),
             pltpu.VMEM((ITERS, 2, rows, lanes), f32),
             pltpu.VMEM((ITERS, 2, rows, lanes), f32),
-            pltpu.VMEM((ITERS, 2, 2, 16, lanes), f32),
             pltpu.VMEM((ITERS, 4, 16, lanes), f32),
-            pltpu.VMEM((ny * nx, 1, lanes), f32),
+            pltpu.VMEM((nx, 1, lanes), f32),
+            pltpu.VMEM((ny, 1, lanes), f32),
             pltpu.SemaphoreType.DMA((2,)),
-            pltpu.SemaphoreType.DMA((ny * nx,)),
-            pltpu.SemaphoreType.DMA((ny * nx,)),
-            pltpu.SemaphoreType.DMA((ITERS, len(DIRS), 4)),
-            pltpu.SemaphoreType.DMA((ITERS, len(DIRS), 4)),
+            pltpu.SemaphoreType.REGULAR((max((ny - 2) // 2, 1),)),
+            pltpu.SemaphoreType.DMA((2, max(ny, nx))),
+            pltpu.SemaphoreType.DMA((2, max(ny, nx))),
+            pltpu.SemaphoreType.DMA((ITERS, len(DIRS), 3)),
+            pltpu.SemaphoreType.DMA((ITERS, len(DIRS), 3)),
         ],
         compiler_params=pltpu.CompilerParams(
             collective_id=0, has_side_effects=True, vmem_limit_bytes=16 * 2**20

time: 26.9 us -> 23.3 us (0.87)
  Pallas kernels: 25.3 us -> 21.7 us
    pallas_call x1, Pallas kernels: 25.3 us -> 21.7 us  [on_device(): pl.pallas_call(functools.partial(kernel, ny, nx), out_shape=jax.ShapeDtyp...]
where the time goes in v2:
time: 23.3 us; the launch traced here: 23.1 us
  Pallas kernels  21.7 us (93%)
  local copies, waits for them, and re-layouts  0.71 us (3%)
  between operations  0.66 us (3%)
    pallas_call x1, Pallas kernels, on_device(): pl.pallas_call(functools.partial(kernel, ny, nx), out_shape=jax.ShapeDtyp...  21.7 us
    unnamed x1, local copies, waits for them, and re-layouts  0.71 us

profile of v2, /device:TPU:0, one launch (start us, length us, event | category | flops | bytes accessed | tf_op | source)
XLA Modules:
  0.0 23.1 jit_solution(4487821676962890444)
XLA Ops:
  0.7 21.7 %shard_map.37 = f32[8,32,256]{2,1,0:T(8,128)S(1)} custom-call(f32[1]{0:T(128)S(6)} %copy.5.smooth_ref, f32[8,32,256]{2,1,0:T(8,128)} %vol_hbm.1, s32[2,4,32]{2,1,0:T(4,128)} %mask_hbm.1), custom_call_target="tpu_custom_call" | custom-call | tf_op jit(solution)/shard_map/pallas_call | solution.py:578
  22.4 0.7 %copy.6 = f32[8,32,256]{2,1,0:T(8,128)} copy(f32[8,32,256]{2,1,0:T(8,128)S(1)} %shard_map.37) | data formatting | bytes 524288

commit v3 on v2

--- a/solution.py
+++ b/solution.py
@@ -88,29 +88,41 @@
             left = jnp.where(group == z, roll(planes[z][:, 0:lanes], 16 * z), left)
         return left, right
 
+    def packed_line(line):
+        match = lane_of(depth) // 16 == lax.broadcasted_iota(jnp.int32, (depth, lanes), 0)
+        ends = []
+        for at, shift in ((0, 0), (cols - lanes, 9)):
+            moved = pltpu.roll(line[:, at : at + lanes], shift, 1, stride=16, stride_axis=0)
+            ends.append(jnp.sum(jnp.where(match, moved, 0.0), axis=0, keepdims=True))
+        return ends
+
     def make_packs(src, it):
         for z in range(depth):
-            row_out[it, 0, z : z + 1] = src[z, rows - 9 : rows - 8, :]
-            row_out[it, 1, z : z + 1] = src[z, 8:9, :]
+            for d, first, ninth in ((0, rows - 1, rows - 9), (1, 0, 8)):
+                row_out[it, d, 0, z : z + 1] = src[z, first : first + 1, :]
+                row_out[it, d, 1, z : z + 1] = src[z, ninth : ninth + 1, :]
         left, right = packed([src[z] for z in range(depth)])
         pack_out[it, 0] = right
         pack_out[it, 1] = left
 
-    def copies(src, it, d):
+    def copies(src, it, d, late):
         dy, dx = DIRS[d]
-        pairs = []
-        if dx == 0:
-            start = rows - 8 if dy > 0 else 0
-            pairs.append((src.at[:, start : start + 8, :], rows_in.at[it, d]))
-            pairs.append((row_out.at[it, d], row_in.at[it, d]))
+        pairs = {}
+        if late:
+            if dx == 0:
+                start = rows - 8 if dy > 0 else 0
+                pairs[2] = (src.at[:, start : start + 8, :], rows_in.at[it, d])
+                pairs[3] = (row_out.at[it, d, 1], row_in.at[it, d, 1])
+        elif dx == 0:
+            pairs[0] = (row_out.at[it, d, 0], row_in.at[it, d, 0])
         elif dy == 0:
-            pairs.append((pack_out.at[it, d - 2], pack_in.at[it, d - 2]))
+            pairs[0] = (pack_out.at[it, d - 2], pack_in.at[it, d - 2])
         else:
             start = rows - 16 if dy > 0 else 0
-            pairs.append((pack_out.at[it, 0 if dx > 0 else 1, start : start + 16], corner_in.at[it, d - 4]))
-        if it == 0:
+            pairs[0] = (pack_out.at[it, 0 if dx > 0 else 1, start : start + 16], corner_in.at[it, d - 4])
+        if it == 0 and not late:
             at = {1: slice(cols - lanes, cols), -1: slice(0, lanes), 0: slice(0, cols)}[dx]
-            pairs.append((own_tiss.at[:, at], near_tiss.at[d, :, at]))
+            pairs[1] = (own_tiss.at[:, at], near_tiss.at[d, :, at])
         return [
             pltpu.make_async_remote_copy(
                 src_ref=a,
@@ -120,7 +132,7 @@
                 device_id={"gy": gy + dy, "gx": gx + dx},
                 device_id_type=MESH,
             )
-            for j, (a, b) in enumerate(pairs)
+            for j, (a, b) in pairs.items()
         ]
 
     def clear_missing(it):
@@ -139,28 +151,30 @@
                     near_tiss[d] = jnp.zeros(near_tiss.shape[1:], jnp.float32)
 
     def start_halo(src, it):
+        for late in (False, True):
+            for d, (dy, dx) in enumerate(DIRS[:2] if late else DIRS):
+
+                @pl.when(exists(dy, dx))
+                def _():
+                    for copy in copies(src, it, d, late):
+                        copy.start()
+
+    def wait_halo(src, it, late):
+        for d, (dy, dx) in enumerate(DIRS[:2] if late else DIRS):
+
+            @pl.when(exists(-dy, -dx))
+            def _():
+                for copy in copies(src, it, d, late):
+                    copy.wait_recv()
+
+    def wait_sent(src, it):
         for d, (dy, dx) in enumerate(DIRS):
 
             @pl.when(exists(dy, dx))
             def _():
-                for copy in copies(src, it, d):
-                    copy.start()
-
-    def wait_halo(src, it):
-        for d, (dy, dx) in enumerate(DIRS):
-
-            @pl.when(exists(-dy, -dx))
-            def _():
-                for copy in copies(src, it, d):
-                    copy.wait_recv()
-
-    def wait_sent(src, it):
-        for d, (dy, dx) in enumerate(DIRS):
-
-            @pl.when(exists(dy, dx))
-            def _():
-                for copy in copies(src, it, d):
-                    copy.wait_send()
+                for late in (False, True):
+                    for copy in copies(src, it, d, late):
+                        copy.wait_send()
 
     def sum_copies(axis):
         count, buffer = (nx, row_sums) if axis == "gx" else (ny, col_sums)
@@ -241,65 +255,77 @@
             for k, part in enumerate(four):
                 vals[k // 2, k % 2, z, PAD : PAD + rows] = part
 
-    def fill_halo(it):
+    def fill_line(it, d, which, corner, at):
+        line = jnp.broadcast_to(corner_in[it, 2 * d + 1, corner : corner + 1], (depth, lanes))
+        extra = pltpu.roll(line, 10, 1, stride=16, stride_axis=0)
+        single = row_in[it, d, which]
+        four = shifted(single[:, 0:lanes], single[:, lanes : 2 * lanes], None)
+        for k, part in enumerate(four):
+            for z in range(depth):
+                row = part[z : z + 1]
+                if k == 3:
+                    row = jnp.where(lane_of(1) < lanes - 6, row, extra[depth - 1 - z : depth - z])
+                vals[k // 2, k % 2, z, at : at + 1] = row
+        fill_packs(
+            at, corner_in[it, 2 * d, corner : corner + 1], packed_line(single),
+            corner_in[it, 2 * d + 1, corner : corner + 1],
+        )
+
+    def fill_early(it):
         lane = lane_of(rows)
         for z in range(depth):
             extra = roll(pack_in[it, 1], lanes - 6 - 16 * z)
             vals[1, 1, z, PAD : PAD + rows] = jnp.where(
                 lane < lanes - 6, vals[1, 1, z, PAD : PAD + rows], extra
             )
-        plane = lax.broadcasted_iota(jnp.int32, (depth, lanes), 0)
-        for d, corner, at, single, alone in (
-            (0, 1, 8, 7, PAD - 9), (1, 3, 0, 8, PAD + rows + 8)
-        ):
+        fill_packs(PAD, pack_in[it, 0], (pack_out[it, 1], pack_out[it, 0]), pack_in[it, 1])
+        fill_line(it, 0, 0, 15, PAD - 1)
+        fill_line(it, 1, 0, 0, PAD + rows)
+        fill_squares()
+
+    def fill_late(it):
+        for d, at, single, alone in ((0, 8, 7, PAD - 9), (1, 0, 8, PAD + rows + 8)):
             start = PAD - 8 if d == 0 else PAD + rows
             for z in range(depth):
-                extra = roll(corner_in[it, corner, at : at + 8], lanes - 6 - 16 * z)
+                extra = roll(corner_in[it, 2 * d + 1, at : at + 8], lanes - 6 - 16 * z)
                 four = shifted(rows_in[it, d, z, :, 0:lanes], rows_in[it, d, z, :, lanes : 2 * lanes], extra)
                 for k, part in enumerate(four):
                     vals[k // 2, k % 2, z, start : start + 8] = part
-            line = jnp.broadcast_to(corner_in[it, corner, single : single + 1], (depth, lanes))
-            extra = jnp.zeros((depth, lanes), jnp.float32)
-            for z in range(depth):
-                extra = jnp.where(plane == z, roll(line, lanes - 6 - 16 * z), extra)
-            four = shifted(row_in[it, d, :, 0:lanes], row_in[it, d, :, lanes : 2 * lanes], extra)
-            for k, part in enumerate(four):
-                for z in range(depth):
-                    vals[k // 2, k % 2, z, alone : alone + 1] = part[z : z + 1]
-        parts = [(PAD, pack_in[it, 0], (pack_out[it, 1], pack_out[it, 0]), pack_in[it, 1])]
-        for d, at, single in ((0, 8, 7), (1, 0, 8)):
-            before, after = corner_in[it, 2 * d], corner_in[it, 2 * d + 1]
-            start = PAD - 8 if d == 0 else PAD + rows
-            alone = PAD - 9 if d == 0 else PAD + rows + 8
-            near = packed([rows_in[it, d, z] for z in range(depth)])
-            line = packed([row_in[it, d, z : z + 1] for z in range(depth)])
-            parts.append((start, before[at : at + 8], near, after[at : at + 8]))
-            parts.append((alone, before[single : single + 1], line, after[single : single + 1]))
-        for start, right_of_left, (left, right), left_of_right in parts:
-            size = left.shape[0]
-            lane = lane_of(size)
-            spot, group = lane % 16, lane // 16
-            zero = jnp.where(
-                spot < 9,
-                right_of_left,
-                jnp.where(
-                    spot < 11, roll(left, 9), jnp.where(spot < 15, roll(right, 6), roll(left_of_right, 15))
-                ),
+            fill_line(it, d, 1, single, alone)
+            fill_packs(
+                start, corner_in[it, 2 * d, at : at + 8], packed([rows_in[it, d, z] for z in range(depth)]),
+                corner_in[it, 2 * d + 1, at : at + 8],
             )
-            eight = jnp.where(
-                spot < 1, roll(right_of_left, -8), jnp.where(spot < 11, roll(left, 1), roll(left_of_right, 7))
-            )
-            hole = jnp.logical_and(group >= 4, group < 7)
-            at = slice(start, start + size)
-            packs[0, at] = zero
-            packs[1, at] = eight
-            packs[2, at] = jnp.where(group == 7, 0.0, zero)
-            packs[3, at] = jnp.where(hole, 0.0, roll(zero, 64))
-            packs[4, at] = jnp.where(hole, 0.0, roll(eight, 64))
-            gap = jnp.logical_and(group >= 1, group < 4)
-            packs[5, at] = jnp.where(group == 0, 0.0, zero)
-            packs[6, at] = jnp.where(gap, 0.0, roll(eight, 64))
-            packs[7, at] = jnp.where(gap, 0.0, roll(zero, 64))
+        fill_squares()
+
+    def fill_packs(start, right_of_left, own, left_of_right):
+        left, right = own
+        size = left.shape[0]
+        lane = lane_of(size)
+        spot, group = lane % 16, lane // 16
+        zero = jnp.where(
+            spot < 9,
+            right_of_left,
+            jnp.where(
+                spot < 11, roll(left, 9), jnp.where(spot < 15, roll(right, 6), roll(left_of_right, 15))
+            ),
+        )
+        eight = jnp.where(
+            spot < 1, roll(right_of_left, -8), jnp.where(spot < 11, roll(left, 1), roll(left_of_right, 7))
+        )
+        hole = jnp.logical_and(group >= 4, group < 7)
+        gap = jnp.logical_and(group >= 1, group < 4)
+        half_zero, half_eight = roll(zero, 64), roll(eight, 64)
+        at = slice(start, start + size)
+        packs[0, at] = zero
+        packs[1, at] = eight
+        packs[2, at] = jnp.where(group == 7, 0.0, zero)
+        packs[3, at] = jnp.where(hole, 0.0, half_zero)
+        packs[4, at] = jnp.where(hole, 0.0, half_eight)
+        packs[5, at] = jnp.where(group == 0, 0.0, zero)
+        packs[6, at] = jnp.where(gap, 0.0, half_eight)
+
+    def fill_squares():
         for t in range(2):
             for ci in range(2):
                 for k in range(2):
@@ -314,10 +340,10 @@
     def add(ref, index, value, init):
         ref[index] = value if init else ref[index] + value
 
-    def box(parts):
+    def box(parts, kind=0):
         tops = [part.astype(jnp.bfloat16).astype(jnp.float32) for part in parts]
         lhs = [jnp.concatenate([top, part - top], axis=1) for part, top in zip(parts, tops)]
-        return jnp.dot(jnp.concatenate(lhs, axis=0), band[...], preferred_element_type=jnp.float32)
+        return jnp.dot(jnp.concatenate(lhs, axis=0), band[kind], preferred_element_type=jnp.float32)
 
     def main_offset(t, offset, init, scale, slot, mode):
         a, b, c = offset
@@ -385,7 +411,7 @@
                 else:
                     gap = diffs[plane][8 : 8 + inner]
                 slot += 1
-                weight = jnp.exp2(penalty - total * scale[0:inner])
+                weight = jnp.exp2(penalty - (total if scale is None else total * scale[0:inner]))
                 push = weight * gap
                 add(acc, (0, 0, t, plane), push[po : po + rows], init)
                 add(acc, (0, 1, t, plane), weight[po : po + rows], init)
@@ -401,11 +427,18 @@
                 totals[t, slot - len(queue) + k, 0:inner] = summed[k * inner : (k + 1) * inner]
         return slot
 
-    def main_gather(t, scale, mode):
-        slot = 0
-        for k, offset in enumerate(LEVEL + CROSS):
-            slot = main_offset(t, offset, k == 0, scale, slot, mode)
-        return 0
+    order = [offset for offset in LEVEL + CROSS if offset[1] == 0]
+    flat = len(order)
+    order += [offset for offset in LEVEL + CROSS if offset[1] != 0]
+    bases = [sum(depth - abs(other[0]) for other in order[:k]) for k in range(len(order))]
+
+    def main_gather(jobs, scale, mode):
+        def body(t, carry):
+            for k in jobs:
+                main_offset(t, order[k], k == 0, scale, bases[k], mode)
+            return carry
+
+        lax.fori_loop(0, 2, body, 0)
 
     packed_items = []
     for a, b, c in LEVEL + CROSS:
@@ -417,19 +450,20 @@
 
     def pack_measure():
         for k, (near, far, b, key, masked) in enumerate(packed_items):
-            k0, k1, lo, size = extent(b)
+            lo, size = extent(b)[2:]
             gap = pack_differ(near, far, b, lo, size)
-            square = gap * gap
-            up, down = roll(square, 16), roll(square, -16)
-            if masked:
-                lane = lane_of(size)
-                up = jnp.where(lane >= 16, up, 0.0)
-                down = jnp.where(lane < lanes - 16, down, 0.0)
-            pcubes[k, 0:size] = square + up + down
-        for k, (near, far, b, key, masked) in enumerate(packed_items):
-            inner = extent(b)[3] - 16
-            total = pcubes[k, 7 : 7 + inner] + pcubes[k, 8 : 8 + inner] + pcubes[k, 9 : 9 + inner]
-            found[k, 0:inner] = total + roll(total, 1) + roll(total, -1)
+            pcubes[k, 0:size] = gap * gap
+        for kind in range(2):
+            chosen = [(k, item) for k, item in enumerate(packed_items) if item[4] == (kind == 0)]
+            parts = []
+            for k, item in chosen:
+                inner = extent(item[2])[3] - 16
+                parts.append(pcubes[k, 7 : 7 + inner] + pcubes[k, 8 : 8 + inner] + pcubes[k, 9 : 9 + inner])
+            pooled = box(parts, 1 + kind)
+            at = 0
+            for (k, item), part in zip(chosen, parts):
+                found[k, 0 : part.shape[0]] = pooled[at : at + part.shape[0]]
+                at += part.shape[0]
 
     def pack_apply(scale):
         parts = [[None] * 4, [None] * 4]
@@ -445,7 +479,8 @@
             k0, k1, lo, size = extent(b)
             bb, inner = b // 8, size - 16
             penalty = ppens[near, 8 * (k0 + 1) : 8 * (k1 + 1)] + ppens[far, 8 * (k0 + bb + 1) : 8 * (k1 + bb + 1)]
-            weight = jnp.exp2(penalty - found[k, 0:inner] * scale[0:inner])
+            total = found[k, 0:inner]
+            weight = jnp.exp2(penalty - (total if scale is None else total * scale[0:inner]))
             push = weight * pack_differ(near, far, b, lo + 8, inner)
             po, qo = -8 * k0, -8 * (bb + k0)
             gain(0, 0, push[po : po + rows], False)
@@ -454,7 +489,7 @@
             gain(1, key, weight[qo : qo + rows], False)
         return parts
 
-    def finish(src, dst, parts):
+    def merge(parts):
         lane = lane_of(rows)
         spot = lane % 16
         merged = []
@@ -465,6 +500,10 @@
             merged.append(
                 jnp.where(jnp.logical_or(spot >= 14, spot == 0), roll(zero, -14), jnp.where(spot < 10, eight, 0.0))
             )
+        return merged
+
+    def finish(src, dst, merged, factor):
+        lane = lane_of(rows)
         for z in range(depth):
             sides = []
             for kind in range(2):
@@ -479,11 +518,18 @@
                 ))
             for t in range(2):
                 at = slice(t * lanes, (t + 1) * lanes)
-                dst[z, :, at] = src[z, :, at] + sides[0][t] / (sides[1][t] + 1.0)
+                dst[z, :, at] = (src[z, :, at] + sides[0][t] / (sides[1][t] + 1.0)) * factor
 
     row_at = lax.broadcasted_iota(jnp.int32, (2 * lanes, lanes), 0) % lanes
     col_at = lax.broadcasted_iota(jnp.int32, (2 * lanes, lanes), 1)
-    band[...] = (jnp.abs(row_at - col_at) <= 1).astype(jnp.float32)
+    beside = jnp.abs(row_at % 16 - col_at % 16) <= 1
+    apart = jnp.abs(row_at // 16 - col_at // 16)
+    for kind, rule in enumerate((
+        jnp.abs(row_at - col_at) <= 1,
+        jnp.logical_and(beside, apart <= 1),
+        jnp.logical_and(beside, jnp.logical_or(apart <= 1, apart == depth - 1)),
+    )):
+        band[kind] = rule.astype(jnp.float32)
     loads[0].wait()
     widen = (
         lax.broadcasted_iota(jnp.int32, (blocks_x, cols), 1) // 8
@@ -535,11 +581,14 @@
     col_sums[0] = functools.reduce(jnp.add, [row_sums[k] for k in range(nx)])
     for copy in sum_copies("gy"):
         copy.start()
-    wait_halo(vol_ref, 0)
+    wait_halo(vol_ref, 0, False)
     spread_tissue()
-    fill_halo(0)
-    lax.fori_loop(0, 2, lambda t, carry: main_gather(t, None, "measure"), 0)
+    fill_early(0)
+    main_gather(range(flat), None, "measure")
+    wait_halo(vol_ref, 0, True)
+    fill_late(0)
     pack_measure()
+    main_gather(range(flat, len(order)), None, "measure")
     for copy in sum_copies("gy"):
         copy.wait_recv()
     everything = functools.reduce(jnp.add, [col_sums[k] for k in range(ny)])
@@ -547,17 +596,25 @@
     tissue_count = everything[:, lanes // 2 : lanes // 2 + 1]
     variance = summed / jnp.maximum(tissue_count, 1.0) + 1e-05
     width = 54.0 * smooth_ref[0] * smooth_ref[0]
-    scale = jnp.broadcast_to(LOG2E / (width * variance), (rows + 8, lanes))
-    lax.fori_loop(0, 2, lambda t, carry: main_gather(t, scale, "apply"), 0)
-    finish(vol_ref, mid, pack_apply(scale))
+    power = LOG2E / (width * variance)
+    scale = jnp.broadcast_to(power, (rows + 8, lanes))
+    root = jnp.broadcast_to(jnp.sqrt(power), (rows, lanes))
+    inverse = jnp.broadcast_to(1.0 / jnp.sqrt(power), (rows, lanes))
+    merged = merge(pack_apply(scale))
+    main_gather(range(len(order)), scale, "apply")
+    finish(vol_ref, mid, merged, root)
     make_packs(mid, 1)
     start_halo(mid, 1)
     fill_own(mid)
-    wait_halo(mid, 1)
-    fill_halo(1)
-    lax.fori_loop(0, 2, lambda t, carry: main_gather(t, scale, "both"), 0)
+    wait_halo(mid, 1, False)
+    fill_early(1)
+    main_gather(range(flat), None, "both")
+    wait_halo(mid, 1, True)
+    fill_late(1)
     pack_measure()
-    finish(mid, out_ref, pack_apply(scale))
+    merged = merge(pack_apply(None))
+    main_gather(range(flat, len(order)), None, "both")
+    finish(mid, out_ref, merged, inverse)
     wait_sent(vol_ref, 0)
     wait_sent(mid, 1)
     for axis in ("gx", "gy"):
@@ -585,11 +642,11 @@
             pltpu.VMEM((blocks_z, blocks_y, blocks_x), jnp.int32),
             pltpu.VMEM((depth, rows, cols), f32),
             pltpu.VMEM((2, 2, depth, rows + 2 * PAD, lanes), f32),
-            pltpu.VMEM((8, rows + 2 * PAD, lanes), f32),
+            pltpu.VMEM((7, rows + 2 * PAD, lanes), f32),
             pltpu.VMEM((2, 2, 2, rows + 2 * PAD, lanes), f32),
             pltpu.VMEM((SLOTS, rows + 24, lanes), f32),
             pltpu.VMEM((2, len(LEVEL) * depth + len(CROSS) * depth // 2, rows + 8, lanes), f32),
-            pltpu.VMEM((2 * lanes, lanes), f32),
+            pltpu.VMEM((3, 2 * lanes, lanes), f32),
             pltpu.VMEM((2, 2, 2, depth, rows, lanes), f32),
             pltpu.VMEM((13, rows + 24, lanes), f32),
             pltpu.VMEM((13, rows + 8, lanes), f32),
@@ -599,8 +656,8 @@
             pltpu.VMEM((len(DIRS), blocks_z * blocks_y, cols), f32),
             pltpu.VMEM((blocks_z, flag_rows, cols + 2 * lanes), f32),
             pltpu.VMEM((ITERS, 2, depth, 8, cols), f32),
-            pltpu.VMEM((ITERS, 2, depth, cols), f32),
-            pltpu.VMEM((ITERS, 2, depth, cols), f32),
+            pltpu.VMEM((ITERS, 2, 2, depth, cols), f32),
+            pltpu.VMEM((ITERS, 2, 2, depth, cols), f32),
             pltpu.VMEM((ITERS, 2, rows, lanes), f32),
             pltpu.VMEM((ITERS, 2, rows, lanes), f32),
             pltpu.VMEM((ITERS, 4, 16, lanes), f32),
@@ -610,8 +667,8 @@
             pltpu.SemaphoreType.REGULAR((max((ny - 2) // 2, 1),)),
             pltpu.SemaphoreType.DMA((2, max(ny, nx))),
             pltpu.SemaphoreType.DMA((2, max(ny, nx))),
-            pltpu.SemaphoreType.DMA((ITERS, len(DIRS), 3)),
-            pltpu.SemaphoreType.DMA((ITERS, len(DIRS), 3)),
+            pltpu.SemaphoreType.DMA((ITERS, len(DIRS), 4)),
+            pltpu.SemaphoreType.DMA((ITERS, len(DIRS), 4)),
         ],
         compiler_params=pltpu.CompilerParams(
             collective_id=0, has_side_effects=True, vmem_limit_bytes=16 * 2**20

time: 23.3 us -> 22.2 us (0.953)
  Pallas kernels: 21.7 us -> 20.6 us
    pallas_call x1, Pallas kernels: 21.7 us -> 20.6 us  [on_device(): pl.pallas_call(functools.partial(kernel, ny, nx), out_shape=jax.ShapeDtyp...]
where the time goes in v3:
time: 22.2 us; the launch traced here: 22 us
  Pallas kernels  20.6 us (93%)
  local copies, waits for them, and re-layouts  0.71 us (3%)
  between operations  0.66 us (3%)
    pallas_call x1, Pallas kernels, on_device(): pl.pallas_call(functools.partial(kernel, ny, nx), out_shape=jax.ShapeDtyp...  20.6 us
    unnamed x1, local copies, waits for them, and re-layouts  0.71 us

profile of v3, /device:TPU:0, one launch (start us, length us, event | category | flops | bytes accessed | tf_op | source)
XLA Modules:
  0.0 22.0 jit_solution(14530356434401843189)
XLA Ops:
  0.7 20.6 %shard_map.37 = f32[8,32,256]{2,1,0:T(8,128)S(1)} custom-call(f32[1]{0:T(128)S(6)} %copy.5.smooth_ref, f32[8,32,256]{2,1,0:T(8,128)} %vol_hbm.1, s32[2,4,32]{2,1,0:T(4,128)} %mask_hbm.1), custom_call_target="tpu_custom_call" | custom-call | tf_op jit(solution)/shard_map/pallas_call | solution.py:635
  21.3 0.7 %copy.6 = f32[8,32,256]{2,1,0:T(8,128)} copy(f32[8,32,256]{2,1,0:T(8,128)S(1)} %shard_map.37) | data formatting | bytes 524288

commit v4 on v3

--- a/solution.py
+++ b/solution.py
@@ -17,7 +17,7 @@
     (4, 0, 8), (4, 8, 8), (4, -8, 8), (-4, 0, 8), (-4, 8, 8), (-4, -8, 8), (4, 0, 0), (4, 8, 0), (4, -8, 0)
 )
 PAD = 16
-SLOTS = 32
+SLOTS = 96
 
 
 def kernel(
@@ -435,7 +435,11 @@
     def main_gather(jobs, scale, mode):
         def body(t, carry):
             for k in jobs:
-                main_offset(t, order[k], k == 0, scale, bases[k], mode)
+                if mode == "both" and k in (2, 4, 6, 8, 10, 12):
+                    main_offset(t, order[k], k == 0, None, bases[k], "measure")
+                    main_offset(t, order[k], k == 0, None, bases[k], "apply")
+                else:
+                    main_offset(t, order[k], k == 0, scale, bases[k], mode)
             return carry
 
         lax.fori_loop(0, 2, body, 0)
@@ -606,6 +610,10 @@
     make_packs(mid, 1)
     start_halo(mid, 1)
     fill_own(mid)
+    wait_sent(vol_ref, 0)
+    for axis in ("gx", "gy"):
+        for copy in sum_copies(axis):
+            copy.wait_send()
     wait_halo(mid, 1, False)
     fill_early(1)
     main_gather(range(flat), None, "both")
@@ -615,11 +623,7 @@
     merged = merge(pack_apply(None))
     main_gather(range(flat, len(order)), None, "both")
     finish(mid, out_ref, merged, inverse)
-    wait_sent(vol_ref, 0)
     wait_sent(mid, 1)
-    for axis in ("gx", "gy"):
-        for copy in sum_copies(axis):
-            copy.wait_send()
 
 
 def on_device(volume, tissue_mask, smoothing):

time: 22.2 us -> 22.2 us (level)
  no operation moved by 1% of the time
where the time goes in v4:
time: 22.2 us; the launch traced here: 22 us
  Pallas kernels  20.6 us (93%)
  local copies, waits for them, and re-layouts  0.71 us (3%)
  between operations  0.66 us (3%)
    pallas_call x1, Pallas kernels, on_device(): pl.pallas_call(functools.partial(kernel, ny, nx), out_shape=jax.ShapeDtyp...  20.6 us
    unnamed x1, local copies, waits for them, and re-layouts  0.71 us

profile of v4, /device:TPU:0, one launch (start us, length us, event | category | flops | bytes accessed | tf_op | source)
XLA Modules:
  0.0 22.0 jit_solution(17415072430644408493)
XLA Ops:
  0.7 20.6 %shard_map.37 = f32[8,32,256]{2,1,0:T(8,128)S(1)} custom-call(f32[1]{0:T(128)S(6)} %copy.5.smooth_ref, f32[8,32,256]{2,1,0:T(8,128)} %vol_hbm.1, s32[2,4,32]{2,1,0:T(4,128)} %mask_hbm.1), custom_call_target="tpu_custom_call" | custom-call | tf_op jit(solution)/shard_map/pallas_call | solution.py:639
  21.3 0.7 %copy.6 = f32[8,32,256]{2,1,0:T(8,128)} copy(f32[8,32,256]{2,1,0:T(8,128)S(1)} %shard_map.37) | data formatting | bytes 524288

commit v5 on v3

--- a/solution.py
+++ b/solution.py
@@ -17,7 +17,7 @@
     (4, 0, 8), (4, 8, 8), (4, -8, 8), (-4, 0, 8), (-4, 8, 8), (-4, -8, 8), (4, 0, 0), (4, 8, 0), (4, -8, 0)
 )
 PAD = 16
-SLOTS = 32
+SLOTS = 96
 
 
 def kernel(
@@ -435,7 +435,11 @@
     def main_gather(jobs, scale, mode):
         def body(t, carry):
             for k in jobs:
-                main_offset(t, order[k], k == 0, scale, bases[k], mode)
+                if mode == "both" and k in (2, 5, 8, 11):
+                    main_offset(t, order[k], k == 0, None, bases[k], "measure")
+                    main_offset(t, order[k], k == 0, None, bases[k], "apply")
+                else:
+                    main_offset(t, order[k], k == 0, scale, bases[k], mode)
             return carry
 
         lax.fori_loop(0, 2, body, 0)

time: 22.2 us -> 22.2 us (level)
  no operation moved by 1% of the time
where the time goes in v5:
time: 22.2 us; the launch traced here: 22 us
  Pallas kernels  20.6 us (93%)
  local copies, waits for them, and re-layouts  0.71 us (3%)
  between operations  0.66 us (3%)
    pallas_call x1, Pallas kernels, on_device(): pl.pallas_call(functools.partial(kernel, ny, nx), out_shape=jax.ShapeDtyp...  20.6 us
    unnamed x1, local copies, waits for them, and re-layouts  0.71 us

profile of v5, /device:TPU:0, one launch (start us, length us, event | category | flops | bytes accessed | tf_op | source)
XLA Modules:
  0.0 22.0 jit_solution(2954146731655710923)
XLA Ops:
  0.7 20.6 %shard_map.37 = f32[8,32,256]{2,1,0:T(8,128)S(1)} custom-call(f32[1]{0:T(128)S(6)} %copy.5.smooth_ref, f32[8,32,256]{2,1,0:T(8,128)} %vol_hbm.1, s32[2,4,32]{2,1,0:T(4,128)} %mask_hbm.1), custom_call_target="tpu_custom_call" | custom-call | tf_op jit(solution)/shard_map/pallas_call | solution.py:639
  21.3 0.7 %copy.6 = f32[8,32,256]{2,1,0:T(8,128)} copy(f32[8,32,256]{2,1,0:T(8,128)S(1)} %shard_map.37) | data formatting | bytes 524288
